TPU v7x, 32 devices: a whole 2x2x4 slice. The times are simulated.
32 devices in a mesh: row: 4 (over x, core), col: 8 (over z, y).
Axes of the slice: x: 2, y: 2, z: 4, core: 2. Of those that a mesh axis runs over, the one named last changes fastest.
Arguments:
- front_panels: float32 [16, 4, 256, 8, 8, 256], P(None, 'row', 'col'), as said below
- child_update_tiles: float32 [4, 8, 8, 256, 256], P('row', 'col'), may hold values from -2 to 2
- child_rows: int32 [4, 8, 8], P('row', 'col'), may hold values from 0 to 63, as said below
- child_cols: int32 [4, 8, 8], P('row', 'col'), may hold values from 0 to 7
- child_counts: int32 [4, 8], P('row', 'col'), may hold values from 4 to 8, as said below
- row_maps: int32 [4, 8, 8, 256], P('row', 'col'), may hold values from 0 to 255, each once within a row
- col_maps: int32 [4, 8, 8, 256], P('row', 'col'), may hold values from 0 to 255, each once within a row
Outputs:
- factored_front: float32 [16, 4, 256, 8, 8, 256], P(None, 'row', None, None, 'col')
Inputs may be any that keep to these rules, and one draw needn't show every extreme that they name: child_rows[r, c, k] modulo 4 names one of four owner rows; among the live slots of one device at most 2 name the same owner row, and some device sends exactly 2 to some owner; every slot's target tile column is at most its target tile row. `child_counts`: every device of col index 0 has all slots live. `front_panels`: the diagonal of the front dominates its first tile, so that tile stays positive definite after the children are added.
All inputs are finite; a program needn't handle non-finite values.
Results may differ from a plain program's by a relative error of at most 0.0003.
Values sent between devices are 32-bit elements; how exact they have to be, the bound alone decides.
No kernel may reach another device: no remote copies, remote signals or barrier semaphores. Data moves between devices by JAX's collectives and lax.ppermute only.
A program may use at most 320 MiB of HBM per device.

v0:
```python
import jax
import jax.numpy as jnp
from jax import lax
from jax.sharding import PartitionSpec as P


def broadcast(value, axis, source):
    kept = jnp.where(lax.axis_index(axis) == source, value, 0).astype(value.dtype)
    return lax.psum(kept, axis)


def slot_positions(owners, is_live):
    slot_entries = owners.shape[-1]
    earlier = lax.broadcasted_iota(
        jnp.int32, (slot_entries, slot_entries), 0
    ) < lax.broadcasted_iota(jnp.int32, (slot_entries, slot_entries), 1)
    same_owner = (owners[..., :, None] == owners[..., None, :]) & is_live[..., :, None] & earlier
    return jnp.sum(same_owner.astype(jnp.int32), axis=-2)


def on_device(
    front_panels, child_update_tiles, child_rows, child_cols, child_counts, row_maps, col_maps
):
    largest_index = lax.Precision.HIGHEST
    row_size = lax.axis_size("row")
    col_size = lax.axis_size("col")
    my_row = lax.axis_index("row")
    my_col = lax.axis_index("col")
    front_width = front_panels.shape[-1]
    blocks = lax.all_to_all(front_panels, "col", split_axis=4, concat_axis=2, tiled=True)
    row_tiles = blocks.shape[0]
    col_tiles = blocks.shape[3]
    blocks = blocks.reshape(row_tiles, front_width, col_tiles, front_width)
    slot_entries = child_update_tiles.shape[2]
    capacity = slot_entries // 4
    labels = lax.broadcasted_iota(jnp.int32, (1, 1, front_width), 2)
    row_indicator = (row_maps.reshape(slot_entries, front_width)[:, :, None] == labels).astype(
        jnp.float32
    )
    column_indicator = (col_maps.reshape(slot_entries, front_width)[:, :, None] == labels).astype(
        jnp.float32
    )
    shifted_tiles = jnp.einsum(
        "gml,gmq->glq",
        row_indicator,
        child_update_tiles.reshape(slot_entries, front_width, front_width),
        precision=largest_index,
    )
    shifted_tiles = jnp.einsum(
        "afb,abx->afx", shifted_tiles, column_indicator, precision=largest_index
    )
    slot_ids = lax.broadcasted_iota(jnp.int32, (slot_entries,), 0)
    is_live = slot_ids < child_counts.reshape(())
    owners = child_rows.reshape(slot_entries) % row_size
    positions = slot_positions(owners, is_live)
    dest_ids = lax.broadcasted_iota(jnp.int32, (row_size, capacity, slot_entries), 0)
    place_ids = lax.broadcasted_iota(jnp.int32, (row_size, capacity, slot_entries), 1)
    selector = (
        (owners[None, None, :] == dest_ids)
        & (positions[None, None, :] == place_ids)
        & is_live[None, None, :]
    ).astype(jnp.float32)
    outgoing = jnp.einsum(
        "opk,kx->opx",
        selector,
        shifted_tiles.reshape(slot_entries, front_width * front_width),
        precision=largest_index,
    )
    incoming = lax.all_to_all(outgoing, "row", split_axis=0, concat_axis=0, tiled=True)
    all_rows, all_cols, all_counts = (
        lax.all_gather(child_rows, "row", axis=0, tiled=True),
        lax.all_gather(child_cols, "row", axis=0, tiled=True),
        lax.all_gather(child_counts, "row", axis=0, tiled=True),
    )
    source_rows = all_rows.reshape(row_size, slot_entries)
    source_cols = all_cols.reshape(row_size, slot_entries)
    source_live = slot_ids[None, :] < all_counts.reshape(row_size)[:, None]
    source_owner = source_rows % row_size
    source_pos = slot_positions(source_owner, source_live)
    mine = (source_live & (source_owner == my_row)).astype(jnp.float32)
    depth_onehot = (
        (source_rows // row_size)[:, :, None]
        == lax.broadcasted_iota(jnp.int32, (1, 1, row_tiles), 2)
    ).astype(jnp.float32) * mine[:, :, None]
    across_onehot = (
        source_cols[:, :, None] == lax.broadcasted_iota(jnp.int32, (1, 1, col_tiles), 2)
    ).astype(jnp.float32)
    place_onehot = (
        source_pos[:, :, None] == lax.broadcasted_iota(jnp.int32, (1, 1, capacity), 2)
    ).astype(jnp.float32)
    landing = jnp.einsum(
        "ska,skb,skp->absp", depth_onehot, across_onehot, place_onehot, precision=largest_index
    )
    incoming = incoming.reshape(row_size, capacity, front_width, front_width)
    blocks = blocks + jnp.einsum("absp,spxy->axby", landing, incoming, precision=largest_index)
    tile_i = lax.broadcasted_iota(jnp.int32, (row_tiles, 1, col_tiles, 1), 0) * row_size + my_row
    tile_j = lax.broadcasted_iota(jnp.int32, (row_tiles, 1, col_tiles, 1), 2) * col_size + my_col
    flipped = jnp.einsum("axby->aybx", blocks)
    blocks = jnp.where(tile_i == tile_j, 0.5 * (blocks + flipped), blocks)
    identity = jnp.eye(front_width, dtype=jnp.float32)
    corner = blocks[0, :, 0, :]
    at_root = (my_row == 0) & (my_col == 0)
    factor = jnp.linalg.cholesky(jnp.where(at_root, corner, identity))
    factor = broadcast(factor, "row", 0)
    column = blocks[:, :, 0, :].reshape(row_tiles * front_width, front_width)
    solved = jax.scipy.linalg.solve_triangular(factor, column.T, lower=True).T.reshape(
        row_tiles, front_width, front_width
    )
    tile_index = lax.broadcasted_iota(jnp.int32, (row_tiles, 1, 1), 0) * row_size + my_row
    kept = jnp.where(tile_index == 0, factor[None, :, :], solved)
    below = jnp.where(tile_index == 0, 0.0, solved)
    row_panel = broadcast(below, "col", 0)
    group = col_size // row_size
    whole = lax.all_gather(row_panel, "row", axis=0, tiled=True)
    whole = whole.reshape(row_size, col_tiles, group, front_width, front_width)
    picked = lax.dynamic_index_in_dim(whole, my_col % row_size, 0, keepdims=False)
    col_panel = lax.dynamic_index_in_dim(picked, my_col // row_size, 1, keepdims=False)
    blocks = blocks - jnp.einsum("asx,bqx->asbq", row_panel, col_panel, precision=largest_index)
    first_column = jnp.where(my_col == 0, kept, blocks[:, :, 0, :])
    blocks = blocks.at[:, :, 0, :].set(first_column)
    blocks = jnp.where(tile_i >= tile_j, blocks, 0.0)
    return blocks.reshape(row_tiles, 1, front_width, col_tiles, 1, front_width)


def solution(mesh):
    return jax.shard_map(
        on_device,
        mesh=mesh,
        in_specs=(
            P(None, "row", "col", None, None, None),
            P("row", "col", None, None, None),
            P("row", "col", None),
            P("row", "col", None),
            P("row", "col"),
            P("row", "col", None, None),
            P("row", "col", None, None),
        ),
        out_specs=P(None, "row", None, None, "col", None),
        check_vma=False,
    )
```

profile of v0, /device:TPU:6, one launch (start us, length us, event | category | flops | bytes accessed | tf_op | source)
XLA Modules:
  0.0 1467.9 jit_solution(9605571834959242759)
XLA Ops:
  23.9 30.6 %copy.67 = f32[16,1,32,8,8,256]{5,3,2,0,1,4:T(8,128)} copy(f32[16,1,32,8,8,256]{5,4,3,2,1,0:T(8,128)} %param.9) | data formatting | bytes 67108864 | tf_op args[0]
  55.8 7.1 all-to-all-start
  83.5 30.9 %convolution_bitcast_fusion = f32[256,256,16,8]{1,2,3,0:T(8,128)} fusion(f32[4,2,256,256,1]{3,2,1,0,4:T(8,128)S(1)} %bitcast.110, f32[16,8,4,2]{0,1,3,2:T(8,128)S(1)} %convolution_bitcast_fusion.1), kind=kOutput, calls=%fused_computation.8 | convolution fusion | flops 805306368 | bytes 35655680 | tf_op jit(solution)/shard_map/absp,spxy->axby/dot_general | solution.py:95
  114.4 34.4 %copy.72 = f32[256,256,16,8]{0,1,3,2:T(8,128)} copy(f32[256,256,16,8]{1,2,3,0:T(8,128)} %convolution_bitcast_fusion) | data formatting | bytes 67108864 | tf_op jit(solution)/shard_map/absp,spxy->axby/dot_general | solution.py:95
  148.9 637.0 %all-to-all-done = f32[16,1,32,8,8,256]{5,3,2,0,1,4:T(8,128)} async-done(((f32[16,1,32,8,8,256]{5,3,2,0,1,4:T(8,128)}), f32[16,1,32,8,8,256]{5,3,2,0,1,4:T(8,128)}, u32[]{:S(2)}, u32[]{:S(2)}) %all-to-all-start) | async-done | bytes 33554464 | tf_op jit(solution)/shard_map/all_to_all | solution.py:30
  785.8 22.9 %copy.68 = f32[16,1,32,8,8,256]{5,3,2,4,0,1:T(8,128)} copy(f32[16,1,32,8,8,256]{5,3,2,0,1,4:T(8,128)} %all-to-all-done) | data formatting | bytes 67108864 | tf_op jit(solution)/shard_map/all_to_all | solution.py:30
  808.7 35.0 %copy.73 = f32[16,256,8,256]{1,3,2,0:T(8,128)} copy(f32[16,256,8,256]{3,2,1,0:T(8,128)} %bitcast.104) | data formatting | bytes 67108864 | tf_op jit(solution)/shard_map/reshape | solution.py:33
  843.7 33.5 %bitcast_add_fusion.1 = f32[16,256,8,256]{1,3,2,0:T(8,128)} fusion(f32[16,256,8,256]{1,3,2,0:T(8,128)} %copy.73, f32[256,256,16,8]{0,1,3,2:T(8,128)} %copy.72), kind=kLoop, calls=%fused_computation.5 | loop fusion | flops 8388608 | bytes 100663296 | tf_op jit(solution)/shard_map/add | solution.py:95
  877.2 31.9 %copy.74 = f32[16,256,8,256]{3,1,2,0:T(8,128)} copy(f32[16,256,8,256]{1,3,2,0:T(8,128)} %bitcast_add_fusion.1) | data formatting | bytes 67108864 | tf_op jit(solution)/shard_map/add | solution.py:95
  909.2 33.6 %fusion.1 = f32[16,256,8,256]{1,3,2,0:T(8,128)} fusion(f32[16,256,8,256]{1,3,2,0:T(8,128)} %bitcast_add_fusion.1, f32[16,256,8,256]{3,1,2,0:T(8,128)} %copy.74, pred[16,8]{1,0:T(8,128)(4,1)S(1)} %get-tuple-element.42), kind=kLoop, calls=%fused_computation.4 | loop fusion | flops 25165824 | bytes 100663424 | tf_op jit(solution)/shard_map/jit(_where)/select_n | solution.py:99
  944.9 11.7 cholesky.50
  956.7 9.8 custom-call.15
  967.0 11.7 cholesky.105
  986.1 5.6 copy.76
  991.7 5.7 copy.77
  997.3 14.2 all-reduce.5.cloned.1.call-done
  1016.4 19.7 %custom-call.16 = f32[2,128,128]{1,2,0:T(8,128)S(1)} custom-call(f32[2,128,128]{2,1,0:T(8,128)S(1)} %get-tuple-element.24), custom_call_target="InvertDiagBlocksLowerTriangular" | custom-call | tf_op jit(solution)/shard_map/jit(_solve_triangular)/triangular_solve | solution.py:106
  1046.0 5.6 copy.94
  1056.4 157.4 %all-reduce.7.cloned.1.call-done = f32[16,256,256]{2,1,0:T(8,128)} async-done(((f32[16,256,256]{2,1,0:T(8,128)}), f32[16,256,256]{2,1,0:T(8,128)}) %all-reduce.7.cloned.1.call-update) | async-done | bytes 4194320 | tf_op jit(solution)/shard_map/psum | solution.py:9
  1213.9 5.6 copy.83
  1219.7 99.9 %all-gather.2.cloned.1.call-done = f32[64,256,256]{2,1,0:T(8,128)} async-done(((f32[16,256,256]{2,1,0:T(8,128)}), f32[64,256,256]{2,1,0:T(8,128)}) %all-gather.2.cloned.1.call-update) | async-done | bytes 16777232 | tf_op jit(solution)/shard_map/all_gather | solution.py:114
  1319.6 35.3 %convolution_subtract_fusion = f32[16,256,8,256]{1,3,2,0:T(8,128)} fusion(f32[16,256,8,256]{1,3,2,0:T(8,128)} %fusion.1, f32[16,256,256]{2,1,0:T(8,128)} %all-reduce.7.cloned.1.call-done, f32[4,8,2,256,256]{4,3,2,1,0:T(8,128)} %bitcast.111, s32[]{:T(128)S(6)} %select_n.139, s32[]{:T(128)S(6)} %select_n.142), kind=kOutput, calls=%fused_computation.7 | convolution fusion | flops 25778192384 | bytes 73400328 | tf_op jit(solution)/shard_map/asx,bqx->asbq/dot_general | solution.py:118
  1359.7 22.9 %select_bitcast_fusion = f32[16,1,256,8,1,256]{2,5,3,0,4,1:T(8,128)} fusion(f32[16,256,8,256]{1,3,2,0:T(8,128)} %fusion.2, pred[16,8]{1,0:T(8,128)(4,1)S(1)} %copy-done.6), kind=kLoop, calls=%fused_computation.6 | loop fusion | flops 8388608 | bytes 67108992 | tf_op jit(solution)/shard_map/reshape | solution.py:122
  1382.6 78.3 %copy.84 = f32[16,1,256,8,1,256]{5,4,3,2,1,0:T(1,128)} copy(f32[16,1,256,8,1,256]{2,5,3,0,4,1:T(8,128)} %select_bitcast_fusion) | data formatting | bytes 67108864 | tf_op jit(solution)/shard_map/reshape | solution.py:122
  (88 shorter events, 75.7 us)
Async XLA Ops:
  6.5 1.6 copy-start
  6.5 3.8 copy-start.7
  19.8 34.7 %all-to-all-start.1 = ((f32[4,2,65536]{2,1,0:T(2,128)}), f32[4,2,65536]{2,1,0:T(2,128)S(1)}, u32[]{:S(2)}, u32[]{:S(2)}) async-start(f32[4,2,65536]{2,1,0:T(2,128)} %fusion.33), calls=%async_computation.1 | async-start | bytes 4194304 | tf_op jit(solution)/shard_map/all_to_all | solution.py:69
  54.5 8.5 copy-start.10
  54.5 13.9 copy-start.8
  54.5 19.0 %copy-start.9 = (s32[1,1,8]{2,1,0:T(1,128)S(1)}, s32[1,1,8]{2,1,0:T(1,128)}, u32[]{:S(2)}) copy-start(s32[1,1,8]{2,1,0:T(1,128)} %param.12) | copy-start | bytes 100
  54.5 1.3 copy-start.4
  55.8 730.0 %all-to-all-start = ((f32[16,1,32,8,8,256]{5,3,2,0,1,4:T(8,128)}), f32[16,1,32,8,8,256]{5,3,2,0,1,4:T(8,128)}, u32[]{:S(2)}, u32[]{:S(2)}) async-start(f32[16,1,32,8,8,256]{5,3,2,0,1,4:T(8,128)} %copy.67), calls=%async_computation | async-start | bytes 67108864 | tf_op jit(solution)/shard_map/all_to_all | solution.py:30
  62.9 948.6 %all-reduce.5.cloned.1.call-start = ((), (), s32[]{:S(2)}) async-start(), calls=%async_computation.2 | async-start | bytes 524288 | tf_op jit(solution)/shard_map/psum | solution.py:9
  981.5 232.4 %all-reduce.7.cloned.1.call-start = ((), (), s32[]{:S(2)}) async-start(), calls=%async_computation.3 | async-start | bytes 8388608 | tf_op jit(solution)/shard_map/psum | solution.py:9
  1036.1 3.7 copy-start.3
  1056.4 263.2 %all-gather.2.cloned.1.call-start = ((), (), s32[]{:S(2)}) async-start(), calls=%async_computation.4 | async-start | bytes 20971520 | tf_op jit(solution)/shard_map/all_gather | solution.py:114
  1213.9 5.6 copy-start.5
  1319.6 35.3 %copy-start.2 = (f32[16,256,1,256]{1,3,2,0:T(8,128)S(1)}, f32[16,256,1,256]{1,3,2,0:T(8,128)}, u32[]{:S(2)}) copy-start(f32[16,256,1,256]{1,3,2,0:T(8,128)} %copy.83) | copy-start | bytes 12582916
  1354.9 4.8 copy-start.6
  1382.6 78.3 %copy-start.1 = (f32[1,1,8,256,256]{4,3,2,1,0:T(8,128)S(1)}, f32[1,1,8,256,256]{4,3,2,1,0:T(8,128)}, u32[]{:S(2)}) copy-start(f32[1,1,8,256,256]{4,3,2,1,0:T(8,128)} %param.10) | copy-start | bytes 6291460
Sparse Core Ops, SparseCore 0:
  981.6 29.8 all-reduce.4
  1056.5 157.3 all-reduce.6
  1215.5 104.0 all-gather.1
where the time goes:
time: 1480 us; the launch traced here: 1470 us
  waiting for transfers between devices  908 us (61%)
  local copies, waits for them, and re-layouts  272 us (18%)
  other arithmetic  162 us (11%)
  matrix products  83.3 us (6%)
  between operations  15.8 us (1%)
  blocking collectives  14.8 us (1%)
    all_to_all x1, waiting for transfers between devices, on_device(): lax.all_to_all(front_panels, 'col', split_axis=4, concat_axis=2, tiled=True)  637 us
    psum x2, waiting for transfers between devices, broadcast(): return lax.psum(kept, axis)  172 us
    all_gather x1, waiting for transfers between devices, on_device(): whole = lax.all_gather(row_panel, 'row', axis=0, tiled=True)  99.9 us
    reshape x1, local copies, waits for them, and re-layouts, on_device(): return blocks.reshape(row_tiles, 1, front_width, col_tiles, 1, front_width)  78.3 us
    dot_general x1, matrix products, on_device(): jnp.einsum('asx,bqx->asbq', row_panel, col_panel, precision=largest_index)  35.3 us
    reshape x1, local copies, waits for them, and re-layouts, on_device(): blocks = blocks.reshape(row_tiles, front_width, col_tiles, front_width)  35 us
    dot_general x1, local copies, waits for them, and re-layouts, on_device(): jnp.einsum('absp,spxy->axby', landing, incoming, precision=largest_index)  34.4 us
    another operation x6, other arithmetic, on_device(): factor = jnp.linalg.cholesky(jnp.where(at_root, corner, identity))  34 us
  transfers between devices with their start and end apart: 5, of which 4 were waited for; matrix products, arithmetic and copies ran while one was open for 8% of the time, Pallas kernels for 0%

commit v1 on v0

v1 whole, which is shorter than its diff:
```python
import functools

import jax
import jax.numpy as jnp
from jax import lax
from jax.experimental import pallas as pl
from jax.experimental.pallas import tpu as pltpu
from jax.sharding import PartitionSpec as P

HIGHEST = lax.Precision.HIGHEST
LANES = 128
VMEM_LIMIT = 48 << 20


def dot_nt(left, right):
    return lax.dot_general(
        left,
        right,
        (((1,), (1,)), ((), ())),
        precision=HIGHEST,
        preferred_element_type=jnp.float32,
    )


def depth_blocks(a, row_size, col_size):
    return (a * row_size + row_size - 1) // col_size + 1


def move_kernel(
    row_size, capacity, ids_ref, rows_ref, count_ref, tiles_ref, row_map_ref, col_map_ref, *out_refs
):
    slots, width = tiles_ref.shape[0], tiles_ref.shape[1]
    labels = lax.broadcasted_iota(jnp.int32, (width, width), 0)
    count = count_ref[0]

    def one(owner, place, out_ref):
        def scan(k, state):
            chosen, seen = state
            hit = (lax.rem(rows_ref[k], row_size) == owner) & (k < count)
            chosen = jnp.where(hit & (seen == place), k, chosen)
            return chosen, seen + hit.astype(jnp.int32)

        chosen, _ = lax.fori_loop(0, slots, scan, (jnp.int32(0), jnp.int32(0)))
        row_hot = (labels == row_map_ref[chosen]).astype(jnp.float32)
        col_hot = (labels == col_map_ref[chosen]).astype(jnp.float32)
        shifted = jnp.dot(
            row_hot, tiles_ref[chosen], precision=HIGHEST, preferred_element_type=jnp.float32
        )
        out_ref[place] = dot_nt(shifted, col_hot)

    for shift, out_ref in enumerate(out_refs):
        owner = lax.rem(ids_ref[0] + shift, row_size)
        for place in range(capacity):
            one(owner, place, out_ref)


def move_tiles(row_size, capacity, ids, rows, count, tiles, row_maps, col_maps):
    slots, width = tiles.shape[0], tiles.shape[1]
    smem = pl.BlockSpec(memory_space=pltpu.SMEM)
    vmem = pl.BlockSpec(memory_space=pltpu.VMEM)
    return pl.pallas_call(
        functools.partial(move_kernel, row_size, capacity),
        out_shape=[jax.ShapeDtypeStruct((capacity, width, width), jnp.float32)] * row_size,
        in_specs=[smem, smem, smem, vmem, vmem, vmem],
        out_specs=[vmem] * row_size,
        compiler_params=pltpu.CompilerParams(vmem_limit_bytes=VMEM_LIMIT),
        name="move_tiles",
    )(ids, rows, count, tiles, row_maps.reshape(slots, 1, width), col_maps.reshape(slots, 1, width))


def locate_kernel(row_size, col_size, capacity, slots, ids_ref, meta_ref, own_ref, lead_ref):
    my_row, my_col = ids_ref[0], ids_ref[1]
    for table, col in ((own_ref, my_col), (lead_ref, 0)):

        def clear(n, carry):
            table[0, n] = -1
            table[1, n] = -1
            return carry

        lax.fori_loop(0, row_size * capacity, clear, 0)

        def source(s, carry):
            line = lax.rem(my_row + row_size - s, row_size) * col_size + col
            count = meta_ref[line, 2 * slots]

            def slot(k, seen):
                target = meta_ref[line, k]
                hit = (lax.rem(target, row_size) == my_row) & (k < count)

                @pl.when(hit)
                def _():
                    table[0, s * capacity + seen] = target // row_size
                    table[1, s * capacity + seen] = meta_ref[line, slots + k]

                return jnp.minimum(seen + hit.astype(jnp.int32), capacity - 1)

            lax.fori_loop(0, slots, slot, jnp.int32(0))
            return carry

        lax.fori_loop(0, row_size, source, 0)


def locate(row_size, col_size, capacity, slots, ids, meta):
    smem = pl.BlockSpec(memory_space=pltpu.SMEM)
    shape = jax.ShapeDtypeStruct((2, row_size * capacity), jnp.int32)
    return pl.pallas_call(
        functools.partial(locate_kernel, row_size, col_size, capacity, slots),
        out_shape=(shape, shape),
        in_specs=[smem, smem],
        out_specs=(smem, smem),
        name="locate",
    )(ids, meta)


def lead_kernel(ids_ref, lead_ref, own_ref, kids_ref, out_ref, corner_ref):
    out_ref[...] = own_ref[...]
    chunk = own_ref.shape[1]
    for n in range(kids_ref.shape[0]):

        @pl.when((lead_ref[0, n] >= 0) & (lead_ref[1, n] == 0))
        def _():
            out_ref[lead_ref[0, n]] += kids_ref[n]

    corner_ref[...] = jnp.zeros_like(corner_ref)

    @pl.when(ids_ref[0] == 0)
    def _():
        start = pl.multiple_of(ids_ref[1] * chunk, chunk)
        corner_ref[pl.ds(start, chunk), :] = out_ref[0]


def lead_rows(ids, lead, own, kids):
    smem = pl.BlockSpec(memory_space=pltpu.SMEM)
    vmem = pl.BlockSpec(memory_space=pltpu.VMEM)
    width = own.shape[2]
    return pl.pallas_call(
        lead_kernel,
        out_shape=(
            jax.ShapeDtypeStruct(own.shape, jnp.float32),
            jax.ShapeDtypeStruct((width, width), jnp.float32),
        ),
        in_specs=[smem, smem, vmem, vmem],
        out_specs=(vmem, vmem),
        compiler_params=pltpu.CompilerParams(vmem_limit_bytes=VMEM_LIMIT),
        name="lead_rows",
    )(ids, lead, own, kids)


def panel_kernel(ids_ref, inverse_ref, factor_ref, rows_ref, cols_ref, row_out, col_out):
    width = inverse_ref.shape[0]
    inverse = inverse_ref[...]

    def row(a, carry):
        row_out[a] = dot_nt(rows_ref[:, a].reshape(width, width), inverse)
        return carry

    lax.fori_loop(0, row_out.shape[0], row, 0)

    @pl.when(ids_ref[0] == 0)
    def _():
        row_out[0] = factor_ref[...]

    def col(b, carry):
        col_out[b] = dot_nt(cols_ref[:, b].reshape(width, width), inverse)
        return carry

    lax.fori_loop(0, col_out.shape[0], col, 0)


def panels(ids, inverse, factor, rows, cols):
    smem = pl.BlockSpec(memory_space=pltpu.SMEM)
    vmem = pl.BlockSpec(memory_space=pltpu.VMEM)
    width = inverse.shape[0]
    return pl.pallas_call(
        panel_kernel,
        out_shape=(
            jax.ShapeDtypeStruct((rows.shape[1], width, width), jnp.float32),
            jax.ShapeDtypeStruct((cols.shape[1], width, width), jnp.float32),
        ),
        in_specs=[smem, vmem, vmem, vmem, vmem],
        out_specs=(vmem, vmem),
        compiler_params=pltpu.CompilerParams(vmem_limit_bytes=VMEM_LIMIT),
        name="panels",
    )(ids, inverse, factor, rows, cols)


def pack_kernel(depths, counts, front_ref, out_ref, in_buf, out_buf, in_sem, out_sem):
    col_size = front_ref.shape[4]
    chunk = front_ref.shape[2]

    def fetch(i):
        a, nb, slot = depths[i], counts[i], i % 2
        return [
            pltpu.make_async_copy(
                front_ref.at[a, 0, :, pl.ds(0, nb), :, pl.ds(half * LANES, LANES)],
                in_buf.at[slot, half, :, pl.ds(0, nb)],
                in_sem.at[slot, half],
            )
            for half in range(2)
        ]

    def send(i):
        first, nb, slot = sum(counts[:i]), counts[i], i % 2
        return pltpu.make_async_copy(
            out_buf.at[slot, :, pl.ds(0, nb)], out_ref.at[:, pl.ds(first, nb)], out_sem.at[slot]
        )

    steps = len(depths)
    for copy in fetch(0):
        copy.start()
    for i in range(steps):
        slot, nb = i % 2, counts[i]
        if i + 1 < steps:
            for copy in fetch(i + 1):
                copy.start()
        for copy in fetch(i):
            copy.wait()
        if i >= 2:
            send(i - 2).wait()
        for half in range(2):
            total = in_buf.shape[3]
            flat = in_buf.at[slot, half].reshape(chunk * total * col_size, LANES)
            for b in range(nb):
                for c in range(col_size):
                    out_buf[slot, c, b, :, half * LANES : (half + 1) * LANES] = flat[
                        pl.ds(b * col_size + c, chunk, stride=total * col_size), :
                    ]
        send(i).start()
    for i in range(max(steps - 2, 0), steps):
        send(i).wait()


def pack(front, depths, counts):
    chunk, col_size, width = front.shape[2], front.shape[4], front.shape[5]
    most = max(counts)
    return pl.pallas_call(
        functools.partial(pack_kernel, depths, counts),
        out_shape=jax.ShapeDtypeStruct((col_size, sum(counts), chunk, width), jnp.float32),
        in_specs=[pl.BlockSpec(memory_space=pltpu.HBM)],
        out_specs=pl.BlockSpec(memory_space=pltpu.HBM),
        scratch_shapes=[
            pltpu.VMEM((2, 2, chunk, most, col_size, LANES), jnp.float32),
            pltpu.VMEM((2, col_size, most, chunk, width), jnp.float32),
            pltpu.SemaphoreType.DMA((2, 2)),
            pltpu.SemaphoreType.DMA((2,)),
        ],
        compiler_params=pltpu.CompilerParams(vmem_limit_bytes=VMEM_LIMIT),
        name="pack",
    )(front)


def finish_kernel(
    depths,
    counts,
    row_size,
    col_size,
    ids_ref,
    own_ref,
    recv_ref,
    rows_ref,
    cols_ref,
    kids_ref,
    *rest,
):
    out_ref, in_buf, row_buf, out_buf, in_sem, row_sem, out_sem = rest[-7:]
    my_row, my_col = ids_ref[0], ids_ref[1]
    width = cols_ref.shape[1]
    chunk = width // col_size
    halves = width // LANES
    blocks = cols_ref.shape[0]
    stride = blocks * halves

    def fetch(i):
        a, nb, slot, first = depths[i], counts[i], i % 2, sum(counts[:i])
        return (
            pltpu.make_async_copy(
                recv_ref.at[:, pl.ds(first, nb)], in_buf.at[slot, :, pl.ds(0, nb)], in_sem.at[slot]
            ),
            pltpu.make_async_copy(rows_ref.at[a], row_buf.at[slot], row_sem.at[slot]),
        )

    def send(i):
        return pltpu.make_async_copy(out_buf.at[i % 2], out_ref.at[depths[i]], out_sem.at[i % 2])

    steps = len(depths)
    for copy in fetch(0):
        copy.start()
    for i in range(steps):
        a, nb, slot = depths[i], counts[i], i % 2
        if i + 1 < steps:
            for copy in fetch(i + 1):
                copy.start()
        for copy in fetch(i):
            copy.wait()
        if i >= 2:
            send(i - 2).wait()
        for n in range(kids_ref.shape[0]):

            @pl.when(own_ref[0, n] == a)
            def _():
                b = own_ref[1, n]
                in_buf[slot, :, b] += kids_ref[n].reshape(col_size, chunk, width)

        tile_i = a * row_size + my_row

        def store(b, tile):
            for half in range(halves):
                out_buf[slot, pl.ds(b * halves + half, width, stride=stride), :] = tile[
                    :, half * LANES : (half + 1) * LANES
                ]

        def update(b):
            return dot_nt(row_buf[slot], cols_ref[b])

        for b in range(nb):
            tile = in_buf[slot, :, b].reshape(width, width)
            tile_j = b * col_size + my_col
            if b < nb - 1:
                store(b, tile - update(b))
            else:

                @pl.when(tile_i > tile_j)
                def _():
                    store(b, tile - update(b))

                @pl.when(tile_i == tile_j)
                def _():
                    store(b, 0.5 * (tile + tile.T) - update(b))

                @pl.when(tile_i < tile_j)
                def _():
                    store(b, jnp.zeros_like(tile))

        @pl.when(my_col == 0)
        def _():
            store(0, row_buf[slot])

        zero = jnp.zeros((width, LANES), jnp.float32)
        for n in range(nb * halves, stride):
            out_buf[slot, pl.ds(n, width, stride=stride), :] = zero
        send(i).start()
    for i in range(max(steps - 2, 0), steps):
        send(i).wait()


def finish(depths, counts, row_size, col_size, ids, own, recv, rows, cols, kids, out=None):
    smem = pl.BlockSpec(memory_space=pltpu.SMEM)
    vmem = pl.BlockSpec(memory_space=pltpu.VMEM)
    hbm = pl.BlockSpec(memory_space=pltpu.HBM)
    blocks, width = cols.shape[0], cols.shape[1]
    chunk = width // col_size
    lines = width * blocks * (width // LANES)
    operands = [ids, own, recv, rows, cols, kids]
    in_specs = [smem, smem, hbm, hbm, vmem, vmem]
    aliases = {}
    if out is not None:
        operands.append(out)
        in_specs.append(hbm)
        aliases = {6: 0}
    return pl.pallas_call(
        functools.partial(finish_kernel, depths, counts, row_size, col_size),
        out_shape=jax.ShapeDtypeStruct((rows.shape[0], lines, LANES), jnp.float32),
        in_specs=in_specs,
        out_specs=hbm,
        scratch_shapes=[
            pltpu.VMEM((2, col_size, max(counts), chunk, width), jnp.float32),
            pltpu.VMEM((2, width, width), jnp.float32),
            pltpu.VMEM((2, lines, LANES), jnp.float32),
            pltpu.SemaphoreType.DMA((2,)),
            pltpu.SemaphoreType.DMA((2,)),
            pltpu.SemaphoreType.DMA((2,)),
        ],
        input_output_aliases=aliases,
        compiler_params=pltpu.CompilerParams(vmem_limit_bytes=VMEM_LIMIT),
        name="finish",
    )(*operands)


def on_device(front, child_tiles, child_rows, child_cols, child_counts, row_maps, col_maps):
    row_size, col_size = lax.axis_size("row"), lax.axis_size("col")
    my_row, my_col = lax.axis_index("row"), lax.axis_index("col")
    row_tiles, chunk, col_tiles, width = front.shape[0], front.shape[2], front.shape[3], front.shape[5]
    slots = child_tiles.shape[2]
    capacity = slots // 4
    arrivals = row_size * capacity
    group = col_size // row_size
    ids = jnp.stack([my_row, my_col]).astype(jnp.int32)

    counts = [depth_blocks(a, row_size, col_size) for a in range(row_tiles)]
    split = row_tiles // 2
    parts = [list(range(row_tiles - 1, split - 1, -1)), list(range(split - 1, -1, -1))]

    packed = [pack(front, part, [counts[a] for a in part]) for part in parts]
    first = lax.all_to_all(packed[0], "col", split_axis=0, concat_axis=0, tiled=True)

    child_tiles, _ = lax.optimization_barrier((child_tiles, packed[0]))
    moved = move_tiles(
        row_size,
        capacity,
        ids,
        child_rows.reshape(slots),
        child_counts.reshape(1),
        child_tiles.reshape(slots, width, width),
        row_maps.reshape(slots, width),
        col_maps.reshape(slots, width),
    )
    meta = jnp.concatenate(
        [child_rows.reshape(1, slots), child_cols.reshape(1, slots), child_counts.reshape(1, 1)], axis=1
    )
    meta = lax.all_gather(meta, ("row", "col"), axis=0, tiled=True)
    own, lead = locate(row_size, col_size, capacity, slots, ids, meta)

    kids = jnp.concatenate(
        [moved[0]]
        + [
            lax.ppermute(moved[shift], "row", [(r, (r + shift) % row_size) for r in range(row_size)])
            for shift in range(1, row_size)
        ]
    )

    pieces = kids.reshape(arrivals, col_size, chunk, width)
    lead_kids = jnp.where(my_col == 0, pieces[:, 0], 0.0)
    for c in range(1, col_size):
        lead_kids = lead_kids + lax.ppermute(pieces[:, c], "col", [(0, c)])
    raw, corner = lead_rows(ids, lead, front[:, 0, :, 0, 0, :], lead_kids)

    corner = lax.psum(corner, ("row", "col"))
    corner = 0.5 * (corner + corner.T)
    factor = jnp.linalg.cholesky(corner)
    inverse = jax.scipy.linalg.solve_triangular(
        factor, jnp.eye(width, dtype=jnp.float32), lower=True
    )

    raw_rows = lax.all_gather(raw, "col", axis=0, tiled=False)
    mine = lax.dynamic_index_in_dim(
        raw_rows.reshape(col_size, col_tiles, group, chunk, width),
        my_col // row_size,
        2,
        keepdims=False,
    )
    raw_cols = jnp.where(my_row == my_col % row_size, mine, 0.0)
    for shift in range(1, row_size):
        pairs = [
            ((c % row_size) * col_size + c, ((c + shift) % row_size) * col_size + c)
            for c in range(col_size)
        ]
        raw_cols = raw_cols + lax.ppermute(mine, ("row", "col"), pairs)
    rows, cols = panels(ids, inverse, factor, raw_rows, raw_cols)

    later, rows, cols = lax.optimization_barrier((packed[1], rows, cols))
    second = lax.all_to_all(later, "col", split_axis=0, concat_axis=0, tiled=True)

    out = None
    for part, recv in zip(parts, (first, second)):
        out = finish(
            part, [counts[a] for a in part], row_size, col_size, ids, own, recv, rows, cols, kids, out
        )
    return out.reshape(row_tiles, 1, width, col_tiles, 1, width)


def solution(mesh):
    return jax.shard_map(
        on_device,
        mesh=mesh,
        in_specs=(
            P(None, "row", "col", None, None, None),
            P("row", "col", None, None, None),
            P("row", "col", None),
            P("row", "col", None),
            P("row", "col"),
            P("row", "col", None, None),
            P("row", "col", None, None),
        ),
        out_specs=P(None, "row", None, None, "col", None),
        check_vma=False,
    )
```

time: 1480 us -> 800 us (0.54)
  waiting for transfers between devices: 908 us -> 343 us
  local copies, waits for them, and re-layouts: 272 us -> 20.8 us
  blocking collectives: 14.8 us -> 225 us
  other arithmetic: 162 us -> 61.2 us
  Pallas kernels: 0 us -> 89.9 us
  matrix products: 83.3 us -> 1.31 us
  starting transfers between devices: 11.3 us -> 28.6 us
    all_to_all x2, waiting for transfers between devices: 637 us -> 90.9 us  [the longest x1 90.9 us: on_device(): lax.all_to_all(later, 'col', split_axis=0, concat_axis=0, tiled=True)]
    all_gather x2 -> x1, blocking collectives: 10.5 us -> 225 us  [on_device(): meta = lax.all_gather(meta, ('row', 'col'), axis=0, tiled=True)]
    reshape x6 -> x0, local copies, waits for them, and re-layouts: 130 us -> none  [the longest x1 78.3 us: on_device(): return blocks.reshape(row_tiles, 1, front_width, col_tiles, 1, front_width)]
    ppermute x0 -> x13, waiting for transfers between devices: none -> 100 us  [the longest x7 75.7 us: on_device(): lead_kids = lead_kids + lax.ppermute(pieces[:, c], 'col', [(0, c)])]
    all_gather x1, waiting for transfers between devices: 99.9 us -> 0.03 us  [on_device(): raw_rows = lax.all_gather(raw, 'col', axis=0, tiled=False)]
    pallas_call x0 -> x8, Pallas kernels: none -> 89.9 us  [the longest x2 40.6 us: finish(): pl.pallas_call(functools.partial(finish_kernel, depths, counts, row_size,...]
    dot_general x6 -> x0, matrix products: 75.3 us -> none  [the longest x1 35.3 us: on_device(): jnp.einsum('asx,bqx->asbq', row_panel, col_panel, precision=largest_index)]
    select_n x7 -> x0, other arithmetic: 40.9 us -> none  [the longest x1 33.6 us: on_device(): blocks = jnp.where(tile_i == tile_j, 0.5 * (blocks + flipped), blocks)]
  transfers between devices with their start and end apart: 5 -> 17, of which waited for: 4 -> 7; matrix products, arithmetic and copies ran while one was open for 8% -> 10% of each run, Pallas kernels for 0% -> 7%
where the time goes in v1:
time: 800 us; the launch traced here: 788 us
  waiting for transfers between devices  343 us (43%)
  blocking collectives  225 us (28%)
  Pallas kernels  89.9 us (11%)
  other arithmetic  61.2 us (8%)
  starting transfers between devices  28.6 us (4%)
  local copies, waits for them, and re-layouts  20.8 us (3%)
  between operations  17.7 us (2%)
    all_gather x1, blocking collectives, on_device(): meta = lax.all_gather(meta, ('row', 'col'), axis=0, tiled=True)  225 us
    psum x1, waiting for transfers between devices, on_device(): corner = lax.psum(corner, ('row', 'col'))  151 us
    all_to_all x1, waiting for transfers between devices, on_device(): lax.all_to_all(later, 'col', split_axis=0, concat_axis=0, tiled=True)  90.9 us
    ppermute x7, waiting for transfers between devices, on_device(): lead_kids = lead_kids + lax.ppermute(pieces[:, c], 'col', [(0, c)])  75.7 us
    pallas_call x2, Pallas kernels, finish(): pl.pallas_call(functools.partial(finish_kernel, depths, counts, row_size,...  40.6 us
    another operation x6, other arithmetic, on_device(): factor = jnp.linalg.cholesky(corner)  34 us
    pallas_call x2, Pallas kernels, pack(): pl.pallas_call(functools.partial(pack_kernel, depths, counts), out_shape=...  21.4 us
    ppermute x3, waiting for transfers between devices, on_device(): lax.ppermute(moved[shift], 'row', [(r, (r + shift) % row_size) for r in r...  21.4 us
  transfers between devices with their start and end apart: 17, of which 7 were waited for; matrix products, arithmetic and copies ran while one was open for 10% of the time, Pallas kernels for 7%

profile of v1, /device:TPU:6, one launch (start us, length us, event | category | flops | bytes accessed | tf_op | source)
XLA Modules:
  0.0 787.9 jit_solution(8467868583272243272)
XLA Ops:
  7.4 14.4 %pack.3 = f32[8,52,32,256]{3,2,1,0:T(8,128)} custom-call(f32[16,1,32,8,8,256]{5,4,3,2,1,0:T(8,128)} %front_ref.3), custom_call_target="tpu_custom_call" | custom-call | tf_op jit(solution)/shard_map/pack/pallas_call | solution.py:236
  21.9 6.5 all-to-all-start.1
  29.3 9.7 %move_tiles.1 = (f32[2,256,256]{2,1,0:T(8,128)S(1)}, f32[2,256,256]{2,1,0:T(8,128)S(1)}, f32[2,256,256]{2,1,0:T(8,128)S(1)}, f32[2,256,256]{2,1,0:T(8,128)S(1)}) custom-call(s32[2]{0:T(128)S(1)} %pad_add_fusion.ids_ref, s32[8]{0:T(128)S(1)} %bitcast.131, s32[1]{0:T(128)} %bitcast.126.count_ref, f32[8,256,256]{2,1,0:T(8,128)S(1)} %bitcast.129, ...), custom_call_target="tpu_custom_call" | custom-call | tf_op jit(solution)/shard_map/move_tiles/pallas_call | solution.py:61
  41.1 11.6 %collective-permute-done = f32[2,256,256]{2,1,0:T(8,128)S(1)} collective-permute-done((f32[2,256,256]{2,1,0:T(8,128)S(1)}, f32[2,256,256]{2,1,0:T(8,128)S(1)}, u32[]{:S(2)}, u32[]{:S(2)}) %collective-permute-start) | collective-permute-done | bytes 524320 | tf_op jit(solution)/shard_map/ppermute | solution.py:416
  54.0 8.6 %collective-permute-done.2 = f32[2,256,256]{2,1,0:T(8,128)S(1)} collective-permute-done((f32[2,256,256]{2,1,0:T(8,128)S(1)}, f32[2,256,256]{2,1,0:T(8,128)S(1)}, u32[]{:S(2)}, u32[]{:S(2)}) %collective-permute-start.2) | collective-permute-done | bytes 524320 | tf_op jit(solution)/shard_map/ppermute | solution.py:416
  69.7 75.7 %collective-permute-done.3 = f32[8,32,256]{2,1,0:T(8,128)S(1)} collective-permute-done((f32[8,32,256]{2,1,0:T(8,128)S(1)}, f32[8,32,256]{2,1,0:T(8,128)S(1)}, u32[]{:S(2)}, u32[]{:S(2)}) %collective-permute-start.3) | collective-permute-done | bytes 262176 | tf_op jit(solution)/shard_map/ppermute | solution.py:424
  148.9 2.5 slice.75
  151.5 225.4 %all-gather.1 = s32[32,1,17]{2,1,0:T(1,128)} all-gather(s32[1,1,17]{2,1,0:T(1,128)S(1)} %add_bitcast_fusion), channel_id=1, replica_groups=mesh['row'=4,'col'=8] {'row','col'}, dimensions={0}, use_global_device_ids=true | all-gather | bytes 2244 | tf_op jit(solution)/shard_map/all_gather | solution.py:410
  377.0 2.8 locate.1
  384.4 7.0 pack.2
  393.7 151.3 %all-reduce.3.cloned.1.call-done = f32[256,256]{0,1:T(8,128)} async-done(((f32[256,256]{0,1:T(8,128)}), f32[256,256]{0,1:T(8,128)}) %all-reduce.3.cloned.1.call-update) | async-done | bytes 262160 | tf_op jit(solution)/shard_map/psum | solution.py:427
  547.3 11.7 %cholesky.50 = f32[128,128]{1,0:T(8,128)S(1)} custom-call(f32[128,128]{1,0:T(8,128)S(1)} %cholesky.118), custom_call_target="Cholesky" | custom-call | tf_op jit(solution)/shard_map/jit(cholesky)/cholesky | solution.py:429
  559.1 9.8 %custom-call.15 = f32[1,128,128]{1,2,0:T(8,128)S(1)} custom-call(f32[1,128,128]{2,1,0:T(8,128)S(1)} %get-tuple-element.63), custom_call_target="InvertDiagBlocksLowerTriangular" | custom-call | tf_op jit(solution)/shard_map/jit(cholesky)/cholesky | solution.py:429
  569.2 3.2 dynamic-slice_bitcast_fusion
  578.4 11.7 %cholesky.105 = f32[128,128]{1,0:T(8,128)S(1)} custom-call(f32[128,128]{1,0:T(8,128)S(1)} %convolution_subtract_fusion.1), custom_call_target="Cholesky" | custom-call | tf_op jit(solution)/shard_map/jit(cholesky)/cholesky | solution.py:429
  592.3 4.2 while.1
  596.5 19.7 %custom-call.16 = f32[2,128,128]{1,2,0:T(8,128)S(1)} custom-call(f32[2,128,128]{2,1,0:T(8,128)S(1)} %get-tuple-element.40), custom_call_target="InvertDiagBlocksLowerTriangular" | custom-call | tf_op jit(solution)/shard_map/jit(_solve_triangular)/triangular_solve | solution.py:430
  617.1 3.3 collective-permute-done.10
  620.4 4.7 add_add_fusion.cols_ref
  625.0 13.9 %panels.1 = (f32[16,256,256]{2,1,0:T(8,128)}, f32[8,256,256]{2,1,0:T(8,128)S(1)}) custom-call(s32[2]{0:T(128)S(1)} %copy-done.6, f32[256,256]{1,0:T(8,128)S(1)} %pad_maximum_fusion.inverse_ref, f32[256,256]{1,0:T(8,128)S(1)} %get-tuple-element.50.factor_ref, f32[8,16,32,256]{3,2,1,0:T(8,128)} %bitcast.135, f32[8,8,32,256]{3,2,1,0:T(8,128)S(1)} %add_add_fusion.cols_ref), custom_call_target="tpu_custom_call" | custom-call | tf_op jit(solution)/shard_map/panels/pallas_call | solution.py:174
  640.3 5.0 all-to-all-start
  646.9 23.0 %finish.2.rest_0_ = f32[16,4096,128]{2,1,0:T(8,128)} custom-call(s32[2]{0:T(128)S(1)} %copy-done.6, s32[2,8]{1,0:T(2,128)S(1)} %copy-done.7, f32[8,52,32,256]{3,2,1,0:T(8,128)} %all-to-all-done.1.recv_ref, f32[16,256,256]{2,1,0:T(8,128)} %get-tuple-element.31.rows_ref, f32[8,256,256]{2,1,0:T(8,128)S(1)} %copy-done.2, ...), custom_call_target="tpu_custom_call" | custom-call | tf_op jit(solution)/shard_map/finish/pallas_call | solution.py:360
  669.9 90.9 %all-to-all-done.recv_ref = f32[8,20,32,256]{3,2,1,0:T(8,128)} async-done(((f32[8,20,32,256]{3,2,1,0:T(8,128)}), f32[8,20,32,256]{3,2,1,0:T(8,128)}, u32[]{:S(2)}, u32[]{:S(2)}) %all-to-all-start) | async-done | bytes 5242912 | tf_op jit(solution)/shard_map/all_to_all | solution.py:451
  762.4 17.5 %finish.3 = f32[16,4096,128]{2,1,0:T(8,128)} custom-call(s32[2]{0:T(128)S(1)} %copy-done.6, s32[2,8]{1,0:T(2,128)S(1)} %copy-done.7, f32[8,20,32,256]{3,2,1,0:T(8,128)} %all-to-all-done.recv_ref, f32[16,256,256]{2,1,0:T(8,128)} %get-tuple-element.31.rows_ref, f32[8,256,256]{2,1,0:T(8,128)S(1)} %copy-done.3, ...), custom_call_target="tpu_custom_call", output_to_operand_aliasing={{}: (6, {})} | custom-call | tf_op jit(solution)/shard_map/finish/pallas_call | solution.py:360
  (97 shorter events, 40.1 us)
Async XLA Ops:
  21.8 7.4 copy-start.12
  21.8 7.4 copy-start.13
  21.8 7.5 copy-start.4
  21.8 7.5 copy-start.8
  21.9 618.5 %all-to-all-start.1 = ((f32[8,52,32,256]{3,2,1,0:T(8,128)}), f32[8,52,32,256]{3,2,1,0:T(8,128)}, u32[]{:S(2)}, u32[]{:S(2)}) async-start(f32[8,52,32,256]{3,2,1,0:T(8,128)} %pack.3), calls=%async_computation.1 | async-start | bytes 27262976 | tf_op jit(solution)/shard_map/all_to_all | solution.py:394
  28.3 516.7 %all-reduce.3.cloned.1.call-start = ((), (), s32[]{:S(2)}) async-start(), calls=%async_computation.2 | async-start | bytes 524288 | tf_op jit(solution)/shard_map/psum | solution.py:427
  29.3 23.4 %copy-start.5 = (s32[2]{0:T(128)}, s32[2]{0:T(128)S(1)}, u32[]{:S(2)}) copy-start(s32[2]{0:T(128)S(1)} %pad_add_fusion.ids_ref) | copy-start | bytes 28
  39.0 13.7 %collective-permute-start = (f32[2,256,256]{2,1,0:T(8,128)S(1)}, f32[2,256,256]{2,1,0:T(8,128)S(1)}, u32[]{:S(2)}, u32[]{:S(2)}) collective-permute-start(f32[2,256,256]{2,1,0:T(8,128)S(1)} %get-tuple-element.23), channel_id=1, source_target_pairs={{0,8},{8,16},{16,24},{24,0},{1,9},{9,17},{17,25},{25,1},{2,10},{10... | collective-permute-start | bytes 1572872 | tf_op jit(solution)/shard_map/ppermute | solution.py:416
  39.1 14.8 %collective-permute-start.1 = (f32[2,256,256]{2,1,0:T(8,128)S(1)}, f32[2,256,256]{2,1,0:T(8,128)S(1)}, u32[]{:S(2)}, u32[]{:S(2)}) collective-permute-start(f32[2,256,256]{2,1,0:T(8,128)S(1)} %get-tuple-element.24), channel_id=1, source_target_pairs={{0,16},{8,24},{16,0},{24,8},{1,17},{9,25},{17,1},{25,9},{2,18},{10... | collective-permute-start | bytes 1572872 | tf_op jit(solution)/shard_map/ppermute | solution.py:416
  39.7 22.9 %collective-permute-start.2 = (f32[2,256,256]{2,1,0:T(8,128)S(1)}, f32[2,256,256]{2,1,0:T(8,128)S(1)}, u32[]{:S(2)}, u32[]{:S(2)}) collective-permute-start(f32[2,256,256]{2,1,0:T(8,128)S(1)} %get-tuple-element.25), channel_id=1, source_target_pairs={{0,24},{8,0},{16,8},{24,16},{1,25},{9,1},{17,9},{25,17},{2,26},{10... | collective-permute-start | bytes 1572872 | tf_op jit(solution)/shard_map/ppermute | solution.py:416
  62.6 88.8 %copy-start.14 = (s32[1,1,8]{2,1,0:T(1,128)S(1)}, s32[1,1,8]{2,1,0:T(1,128)}, u32[]{:S(2)}) copy-start(s32[1,1,8]{2,1,0:T(1,128)} %param.10) | copy-start | bytes 100
  63.6 81.7 %collective-permute-start.3 = (f32[8,32,256]{2,1,0:T(8,128)S(1)}, f32[8,32,256]{2,1,0:T(8,128)S(1)}, u32[]{:S(2)}, u32[]{:S(2)}) collective-permute-start(f32[8,32,256]{2,1,0:T(8,128)S(1)} %get-tuple-element.53), channel_id=1, source_target_pairs={{0,1},{8,9},{16,17},{24,25}} | collective-permute-start | bytes 786440 | tf_op jit(solution)/shard_map/ppermute | solution.py:424
  64.9 81.8 %collective-permute-start.8 = (f32[8,32,256]{2,1,0:T(8,128)S(1)}, f32[8,32,256]{2,1,0:T(8,128)S(1)}, u32[]{:S(2)}, u32[]{:S(2)}) collective-permute-start(f32[8,32,256]{2,1,0:T(8,128)S(1)} %get-tuple-element.54), channel_id=1, source_target_pairs={{0,6},{8,14},{16,22},{24,30}} | collective-permute-start | bytes 786440 | tf_op jit(solution)/shard_map/ppermute | solution.py:424
  65.6 314.3 %collective-permute-start.7 = (f32[8,32,256]{2,1,0:T(8,128)}, f32[8,32,256]{2,1,0:T(8,128)}, u32[]{:S(2)}, u32[]{:S(2)}) collective-permute-start(f32[8,32,256]{2,1,0:T(8,128)} %get-tuple-element.55), channel_id=1, source_target_pairs={{0,5},{8,13},{16,21},{24,29}} | collective-permute-start | bytes 786440 | tf_op jit(solution)/shard_map/ppermute | solution.py:424
  67.0 312.9 %collective-permute-start.6 = (f32[8,32,256]{2,1,0:T(8,128)}, f32[8,32,256]{2,1,0:T(8,128)}, u32[]{:S(2)}, u32[]{:S(2)}) collective-permute-start(f32[8,32,256]{2,1,0:T(8,128)} %get-tuple-element.56), channel_id=1, source_target_pairs={{0,4},{8,12},{16,20},{24,28}} | collective-permute-start | bytes 786440 | tf_op jit(solution)/shard_map/ppermute | solution.py:424
  68.3 311.5 %collective-permute-start.5 = (f32[8,32,256]{2,1,0:T(8,128)S(1)}, f32[8,32,256]{2,1,0:T(8,128)}, u32[]{:S(2)}, u32[]{:S(2)}) collective-permute-start(f32[8,32,256]{2,1,0:T(8,128)S(1)} %get-tuple-element.57), channel_id=1, source_target_pairs={{0,3},{8,11},{16,19},{24,27}} | collective-permute-start | bytes 786440 | tf_op jit(solution)/shard_map/ppermute | solution.py:424
  145.4 234.5 %collective-permute-start.4 = (f32[8,32,256]{2,1,0:T(8,128)S(1)}, f32[8,32,256]{2,1,0:T(8,128)}, u32[]{:S(2)}, u32[]{:S(2)}) collective-permute-start(f32[8,32,256]{2,1,0:T(8,128)S(1)} %get-tuple-element.58), channel_id=1, source_target_pairs={{0,2},{8,10},{16,18},{24,26}} | collective-permute-start | bytes 786440 | tf_op jit(solution)/shard_map/ppermute | solution.py:424
  147.4 234.0 %copy-start.6 = (s32[2]{0:T(128)S(1)}, s32[2]{0:T(128)}, u32[]{:S(2)}) copy-start(s32[2]{0:T(128)} %copy-done.5) | copy-start | bytes 28
  147.4 232.5 %collective-permute-start.9 = (f32[8,32,256]{2,1,0:T(8,128)S(1)}, f32[8,32,256]{2,1,0:T(8,128)}, u32[]{:S(2)}, u32[]{:S(2)}) collective-permute-start(f32[8,32,256]{2,1,0:T(8,128)S(1)} %get-tuple-element.59), channel_id=1, source_target_pairs={{0,7},{8,15},{16,23},{24,31}} | collective-permute-start | bytes 786440 | tf_op jit(solution)/shard_map/ppermute | solution.py:424
  383.8 185.3 %all-gather.4.cloned.1.call-start = ((), (), s32[]{:S(2)}) async-start(), calls=%async_computation.3 | async-start | bytes 4718592 | tf_op jit(solution)/shard_map/all_gather | solution.py:434
  572.4 44.7 %collective-permute-start.11 = (f32[8,8,32,256]{3,2,1,0:T(8,128)}, f32[8,8,32,256]{3,2,1,0:T(8,128)}, u32[]{:S(2)}, u32[]{:S(2)}) collective-permute-start(f32[8,8,32,256]{3,2,1,0:T(8,128)} %dynamic-slice_bitcast_fusion), channel_id=1, source_target_pairs={{0,16},{9,25},{18,2},{27,11},{4,20},{13,29},{22,6},{31,15}} | collective-permute-start | bytes 6291464 | tf_op jit(solution)/shard_map/ppermute | solution.py:447
  574.4 45.9 %collective-permute-start.10 = (f32[8,8,32,256]{3,2,1,0:T(8,128)}, f32[8,8,32,256]{3,2,1,0:T(8,128)}, u32[]{:S(2)}, u32[]{:S(2)}) collective-permute-start(f32[8,8,32,256]{3,2,1,0:T(8,128)} %dynamic-slice_bitcast_fusion), channel_id=1, source_target_pairs={{0,8},{9,17},{18,26},{27,3},{4,12},{13,21},{22,30},{31,7}} | collective-permute-start | bytes 6291464 | tf_op jit(solution)/shard_map/ppermute | solution.py:447
  575.7 44.6 %collective-permute-start.12 = (f32[8,8,32,256]{3,2,1,0:T(8,128)}, f32[8,8,32,256]{3,2,1,0:T(8,128)}, u32[]{:S(2)}, u32[]{:S(2)}) collective-permute-start(f32[8,8,32,256]{3,2,1,0:T(8,128)} %dynamic-slice_bitcast_fusion), channel_id=1, source_target_pairs={{0,24},{9,1},{18,10},{27,19},{4,28},{13,5},{22,14},{31,23}} | collective-permute-start | bytes 6291464 | tf_op jit(solution)/shard_map/ppermute | solution.py:447
  640.3 120.5 %all-to-all-start = ((f32[8,20,32,256]{3,2,1,0:T(8,128)}), f32[8,20,32,256]{3,2,1,0:T(8,128)}, u32[]{:S(2)}, u32[]{:S(2)}) async-start(f32[8,20,32,256]{3,2,1,0:T(8,128)} %copy-done), calls=%async_computation | async-start | bytes 10485760 | tf_op jit(solution)/shard_map/all_to_all | solution.py:451
  (8 other events, 15.6 us)
Sparse Core Ops, SparseCore 0:
  383.9 161.0 all-reduce.2
Sparse Core Ops, SparseCore 1:
  386.4 72.7 all-gather.3

commit v2 on v1

--- a/solution.py
+++ b/solution.py
@@ -9,7 +9,7 @@
 
 HIGHEST = lax.Precision.HIGHEST
 LANES = 128
-VMEM_LIMIT = 48 << 20
+VMEM_LIMIT = 60 << 20
 
 
 def dot_nt(left, right):
@@ -22,131 +22,193 @@
     )
 
 
+def bf16_nt(left, right):
+    return lax.dot_general(
+        left, right, (((1,), (1,)), ((), ())), preferred_element_type=jnp.float32
+    )
+
+
 def depth_blocks(a, row_size, col_size):
     return (a * row_size + row_size - 1) // col_size + 1
 
 
 def move_kernel(
-    row_size, capacity, ids_ref, rows_ref, count_ref, tiles_ref, row_map_ref, col_map_ref, *out_refs
+    row_size,
+    capacity,
+    ids_ref,
+    rows_ref,
+    cols_ref,
+    count_ref,
+    tiles_ref,
+    row_map_ref,
+    col_map_ref,
+    *out_refs,
 ):
     slots, width = tiles_ref.shape[0], tiles_ref.shape[1]
+    out_refs, lead_refs = out_refs[:row_size], out_refs[row_size:]
+    chunk = width // len(lead_refs)
     labels = lax.broadcasted_iota(jnp.int32, (width, width), 0)
     count = count_ref[0]
 
-    def one(owner, place, out_ref):
+    def one(shift, place, out_ref):
+        owner = lax.rem(ids_ref[0] + shift, row_size)
         def scan(k, state):
             chosen, seen = state
             hit = (lax.rem(rows_ref[k], row_size) == owner) & (k < count)
             chosen = jnp.where(hit & (seen == place), k, chosen)
             return chosen, seen + hit.astype(jnp.int32)
 
-        chosen, _ = lax.fori_loop(0, slots, scan, (jnp.int32(0), jnp.int32(0)))
+        chosen, seen = lax.fori_loop(0, slots, scan, (jnp.int32(0), jnp.int32(0)))
         row_hot = (labels == row_map_ref[chosen]).astype(jnp.float32)
         col_hot = (labels == col_map_ref[chosen]).astype(jnp.float32)
         shifted = jnp.dot(
             row_hot, tiles_ref[chosen], precision=HIGHEST, preferred_element_type=jnp.float32
         )
-        out_ref[place] = dot_nt(shifted, col_hot)
+        tile = dot_nt(shifted, col_hot)
+        out_ref[place] = tile
+        here = (seen > place) & (cols_ref[chosen] == 0)
+        target = jnp.where(here, rows_ref[chosen] // row_size, -1).astype(jnp.float32)
+        for c, lead_ref in enumerate(lead_refs):
+            lead_ref[shift, pl.ds(place * chunk, chunk), :] = tile[c * chunk : (c + 1) * chunk]
+            lead_ref[shift, pl.ds(capacity * chunk + place * 8, 8), :] = jnp.full(
+                (8, width), target
+            )
 
     for shift, out_ref in enumerate(out_refs):
-        owner = lax.rem(ids_ref[0] + shift, row_size)
         for place in range(capacity):
-            one(owner, place, out_ref)
-
-
-def move_tiles(row_size, capacity, ids, rows, count, tiles, row_maps, col_maps):
+            one(shift, place, out_ref)
+
+
+def move_tiles(row_size, col_size, capacity, ids, rows, cols, count, tiles, row_maps, col_maps):
     slots, width = tiles.shape[0], tiles.shape[1]
     smem = pl.BlockSpec(memory_space=pltpu.SMEM)
     vmem = pl.BlockSpec(memory_space=pltpu.VMEM)
     return pl.pallas_call(
         functools.partial(move_kernel, row_size, capacity),
-        out_shape=[jax.ShapeDtypeStruct((capacity, width, width), jnp.float32)] * row_size,
-        in_specs=[smem, smem, smem, vmem, vmem, vmem],
-        out_specs=[vmem] * row_size,
+        out_shape=[jax.ShapeDtypeStruct((capacity, width, width), jnp.float32)] * row_size
+        + [
+            jax.ShapeDtypeStruct((row_size, capacity * (width // col_size + 8), width), jnp.float32)
+        ]
+        * col_size,
+        in_specs=[smem, smem, smem, smem, vmem, vmem, vmem],
+        out_specs=[vmem] * (row_size + col_size),
         compiler_params=pltpu.CompilerParams(vmem_limit_bytes=VMEM_LIMIT),
         name="move_tiles",
-    )(ids, rows, count, tiles, row_maps.reshape(slots, 1, width), col_maps.reshape(slots, 1, width))
-
-
-def locate_kernel(row_size, col_size, capacity, slots, ids_ref, meta_ref, own_ref, lead_ref):
-    my_row, my_col = ids_ref[0], ids_ref[1]
-    for table, col in ((own_ref, my_col), (lead_ref, 0)):
-
-        def clear(n, carry):
-            table[0, n] = -1
-            table[1, n] = -1
-            return carry
-
-        lax.fori_loop(0, row_size * capacity, clear, 0)
-
-        def source(s, carry):
-            line = lax.rem(my_row + row_size - s, row_size) * col_size + col
-            count = meta_ref[line, 2 * slots]
-
-            def slot(k, seen):
-                target = meta_ref[line, k]
-                hit = (lax.rem(target, row_size) == my_row) & (k < count)
-
-                @pl.when(hit)
-                def _():
-                    table[0, s * capacity + seen] = target // row_size
-                    table[1, s * capacity + seen] = meta_ref[line, slots + k]
-
-                return jnp.minimum(seen + hit.astype(jnp.int32), capacity - 1)
-
-            lax.fori_loop(0, slots, slot, jnp.int32(0))
-            return carry
-
-        lax.fori_loop(0, row_size, source, 0)
-
-
-def locate(row_size, col_size, capacity, slots, ids, meta):
+    )(ids, rows, cols, count, tiles, row_maps.reshape(slots, 1, width), col_maps.reshape(slots, 1, width))
+
+
+def locate_kernel(row_size, capacity, slots, ids_ref, meta_ref, own_ref):
+    my_row = ids_ref[0]
+
+    def clear(n, carry):
+        own_ref[0, n] = -1
+        own_ref[1, n] = -1
+        return carry
+
+    lax.fori_loop(0, row_size * capacity, clear, 0)
+
+    def source(s, carry):
+        line = lax.rem(my_row + row_size - s, row_size)
+        count = meta_ref[line, 2 * slots]
+
+        def slot(k, seen):
+            target = meta_ref[line, k]
+            hit = (lax.rem(target, row_size) == my_row) & (k < count)
+
+            @pl.when(hit)
+            def _():
+                own_ref[0, s * capacity + seen] = target // row_size
+                own_ref[1, s * capacity + seen] = meta_ref[line, slots + k]
+
+            return jnp.minimum(seen + hit.astype(jnp.int32), capacity - 1)
+
+        lax.fori_loop(0, slots, slot, jnp.int32(0))
+        return carry
+
+    lax.fori_loop(0, row_size, source, 0)
+
+
+def locate(row_size, capacity, slots, ids, meta):
     smem = pl.BlockSpec(memory_space=pltpu.SMEM)
-    shape = jax.ShapeDtypeStruct((2, row_size * capacity), jnp.int32)
-    return pl.pallas_call(
-        functools.partial(locate_kernel, row_size, col_size, capacity, slots),
-        out_shape=(shape, shape),
+    return pl.pallas_call(
+        functools.partial(locate_kernel, row_size, capacity, slots),
+        out_shape=jax.ShapeDtypeStruct((2, row_size * capacity), jnp.int32),
         in_specs=[smem, smem],
-        out_specs=(smem, smem),
+        out_specs=smem,
         name="locate",
     )(ids, meta)
 
 
-def lead_kernel(ids_ref, lead_ref, own_ref, kids_ref, out_ref, corner_ref):
-    out_ref[...] = own_ref[...]
-    chunk = own_ref.shape[1]
-    for n in range(kids_ref.shape[0]):
-
-        @pl.when((lead_ref[0, n] >= 0) & (lead_ref[1, n] == 0))
-        def _():
-            out_ref[lead_ref[0, n]] += kids_ref[n]
-
-    corner_ref[...] = jnp.zeros_like(corner_ref)
-
-    @pl.when(ids_ref[0] == 0)
-    def _():
-        start = pl.multiple_of(ids_ref[1] * chunk, chunk)
-        corner_ref[pl.ds(start, chunk), :] = out_ref[0]
-
-
-def lead_rows(ids, lead, own, kids):
+def lead_kernel(capacity, front_ref, *refs):
+    kids_refs, (out_ref, buf, sem) = refs[:-3], refs[-3:]
+    row_tiles, chunk, col_size = front_ref.shape[0], front_ref.shape[2], front_ref.shape[4]
+    copies = [
+        pltpu.make_async_copy(
+            front_ref.at[:, 0, :, 0, :, pl.ds(half * LANES, LANES)], buf.at[half], sem.at[half]
+        )
+        for half in range(2)
+    ]
+    for copy in copies:
+        copy.start()
+    for copy in copies:
+        copy.wait()
+    for half in range(2):
+        flat = buf.at[half].reshape(row_tiles * chunk * col_size, LANES)
+        for a in range(row_tiles):
+            out_ref[a, :, half * LANES : (half + 1) * LANES] = flat[
+                pl.ds(a * chunk * col_size, chunk, stride=col_size), :
+            ]
+    for kids_ref in kids_refs:
+        for place in range(capacity):
+            kid = kids_ref[pl.ds(place * chunk, chunk), :]
+            target = kids_ref[pl.ds(capacity * chunk + place * 8, 1), :]
+            for a in range(row_tiles):
+                out_ref[a] += jnp.where(target == a, kid, 0.0)
+
+
+def lead_rows(capacity, front, kids):
+    vmem = pl.BlockSpec(memory_space=pltpu.VMEM)
+    row_tiles, chunk, col_size, width = front.shape[0], front.shape[2], front.shape[4], front.shape[5]
+    return pl.pallas_call(
+        functools.partial(lead_kernel, capacity),
+        out_shape=jax.ShapeDtypeStruct((row_tiles, chunk, width), jnp.float32),
+        in_specs=[pl.BlockSpec(memory_space=pltpu.HBM)] + [vmem] * len(kids),
+        out_specs=vmem,
+        scratch_shapes=[
+            pltpu.VMEM((2, row_tiles, chunk, col_size, LANES), jnp.float32),
+            pltpu.SemaphoreType.DMA((2,)),
+        ],
+        compiler_params=pltpu.CompilerParams(vmem_limit_bytes=VMEM_LIMIT),
+        name="lead_rows",
+    )(front, *kids)
+
+
+def order_kernel(ids_ref, *refs):
+    same, other_ref, out_ref = refs[:-2], refs[-2], refs[-1]
+    for k, same_ref in enumerate(same):
+        out_ref[lax.bitwise_xor(ids_ref[1], 2 * k)] = same_ref[...]
+        out_ref[lax.bitwise_xor(ids_ref[1], 2 * k + 1)] = other_ref[k]
+
+
+def order_rows(ids, same, other):
     smem = pl.BlockSpec(memory_space=pltpu.SMEM)
     vmem = pl.BlockSpec(memory_space=pltpu.VMEM)
-    width = own.shape[2]
-    return pl.pallas_call(
-        lead_kernel,
-        out_shape=(
-            jax.ShapeDtypeStruct(own.shape, jnp.float32),
-            jax.ShapeDtypeStruct((width, width), jnp.float32),
-        ),
-        in_specs=[smem, smem, vmem, vmem],
-        out_specs=(vmem, vmem),
+    return pl.pallas_call(
+        order_kernel,
+        out_shape=jax.ShapeDtypeStruct((2 * len(same),) + same[0].shape, jnp.float32),
+        in_specs=[smem] + [vmem] * (1 + len(same)),
+        out_specs=vmem,
         compiler_params=pltpu.CompilerParams(vmem_limit_bytes=VMEM_LIMIT),
-        name="lead_rows",
-    )(ids, lead, own, kids)
-
-
-def panel_kernel(ids_ref, inverse_ref, factor_ref, rows_ref, cols_ref, row_out, col_out):
+        name="order_rows",
+    )(ids, *same, other)
+
+
+def halves_of(value):
+    high = value.astype(jnp.bfloat16)
+    return high, (value - high.astype(jnp.float32)).astype(jnp.bfloat16)
+
+
+def panel_kernel(ids_ref, inverse_ref, factor_ref, rows_ref, cols_ref, row_out, high_out, low_out):
     width = inverse_ref.shape[0]
     inverse = inverse_ref[...]
 
@@ -160,11 +222,12 @@
     def _():
         row_out[0] = factor_ref[...]
 
-    def col(b, carry):
-        col_out[b] = dot_nt(cols_ref[:, b].reshape(width, width), inverse)
+    def column(b, carry):
+        col = dot_nt(cols_ref[:, b].reshape(width, width), inverse)
+        high_out[b], low_out[b] = halves_of(col)
         return carry
 
-    lax.fori_loop(0, col_out.shape[0], col, 0)
+    lax.fori_loop(0, high_out.shape[0], column, 0)
 
 
 def panels(ids, inverse, factor, rows, cols):
@@ -175,10 +238,11 @@
         panel_kernel,
         out_shape=(
             jax.ShapeDtypeStruct((rows.shape[1], width, width), jnp.float32),
-            jax.ShapeDtypeStruct((cols.shape[1], width, width), jnp.float32),
+            jax.ShapeDtypeStruct((cols.shape[1], width, width), jnp.bfloat16),
+            jax.ShapeDtypeStruct((cols.shape[1], width, width), jnp.bfloat16),
         ),
         in_specs=[smem, vmem, vmem, vmem, vmem],
-        out_specs=(vmem, vmem),
+        out_specs=(vmem, vmem, vmem),
         compiler_params=pltpu.CompilerParams(vmem_limit_bytes=VMEM_LIMIT),
         name="panels",
     )(ids, inverse, factor, rows, cols)
@@ -258,16 +322,17 @@
     own_ref,
     recv_ref,
     rows_ref,
-    cols_ref,
+    high_ref,
+    low_ref,
     kids_ref,
     *rest,
 ):
     out_ref, in_buf, row_buf, out_buf, in_sem, row_sem, out_sem = rest[-7:]
     my_row, my_col = ids_ref[0], ids_ref[1]
-    width = cols_ref.shape[1]
+    width = high_ref.shape[1]
     chunk = width // col_size
     halves = width // LANES
-    blocks = cols_ref.shape[0]
+    blocks = high_ref.shape[0]
     stride = blocks * halves
 
     def fetch(i):
@@ -309,8 +374,12 @@
                     :, half * LANES : (half + 1) * LANES
                 ]
 
+        row_high, row_low = halves_of(row_buf[slot])
+
         def update(b):
-            return dot_nt(row_buf[slot], cols_ref[b])
+            return bf16_nt(row_high, high_ref[b]) + (
+                bf16_nt(row_high, low_ref[b]) + bf16_nt(row_low, high_ref[b])
+            )
 
         for b in range(nb):
             tile = in_buf[slot, :, b].reshape(width, width)
@@ -343,20 +412,20 @@
         send(i).wait()
 
 
-def finish(depths, counts, row_size, col_size, ids, own, recv, rows, cols, kids, out=None):
+def finish(depths, counts, row_size, col_size, ids, own, recv, rows, high, low, kids, out=None):
     smem = pl.BlockSpec(memory_space=pltpu.SMEM)
     vmem = pl.BlockSpec(memory_space=pltpu.VMEM)
     hbm = pl.BlockSpec(memory_space=pltpu.HBM)
-    blocks, width = cols.shape[0], cols.shape[1]
+    blocks, width = high.shape[0], high.shape[1]
     chunk = width // col_size
     lines = width * blocks * (width // LANES)
-    operands = [ids, own, recv, rows, cols, kids]
-    in_specs = [smem, smem, hbm, hbm, vmem, vmem]
+    operands = [ids, own, recv, rows, high, low, kids]
+    in_specs = [smem, smem, hbm, hbm, vmem, vmem, vmem]
     aliases = {}
     if out is not None:
         operands.append(out)
         in_specs.append(hbm)
-        aliases = {6: 0}
+        aliases = {7: 0}
     return pl.pallas_call(
         functools.partial(finish_kernel, depths, counts, row_size, col_size),
         out_shape=jax.ShapeDtypeStruct((rows.shape[0], lines, LANES), jnp.float32),
@@ -387,51 +456,80 @@
     ids = jnp.stack([my_row, my_col]).astype(jnp.int32)
 
     counts = [depth_blocks(a, row_size, col_size) for a in range(row_tiles)]
-    split = row_tiles // 2
-    parts = [list(range(row_tiles - 1, split - 1, -1)), list(range(split - 1, -1, -1))]
-
-    packed = [pack(front, part, [counts[a] for a in part]) for part in parts]
-    first = lax.all_to_all(packed[0], "col", split_axis=0, concat_axis=0, tiled=True)
-
-    child_tiles, _ = lax.optimization_barrier((child_tiles, packed[0]))
+    parts = [[row_tiles - 2], [row_tiles - 1, row_tiles - 3, row_tiles - 4]]
+    last = (row_tiles - 5) * 3 // 4
+    parts.append([a for a in range(row_tiles - 5, -1, -1) if a != last])
+    parts.append([last])
+
+    def exchange(part, *after):
+        blocks = pack(front, part, [counts[a] for a in part])
+        blocks = lax.optimization_barrier((blocks,) + after)[0]
+        return lax.all_to_all(blocks, "col", split_axis=0, concat_axis=0, tiled=True)
+
+    def along_row(shift):
+        return [(r, (r + shift) % row_size) for r in range(row_size)]
+
+    def across_col(k):
+        return [(c, c ^ k) for c in range(col_size)]
+
     moved = move_tiles(
         row_size,
+        col_size,
         capacity,
         ids,
         child_rows.reshape(slots),
+        child_cols.reshape(slots),
         child_counts.reshape(1),
         child_tiles.reshape(slots, width, width),
         row_maps.reshape(slots, width),
         col_maps.reshape(slots, width),
     )
+    moved, pieces = moved[:row_size], moved[row_size:]
+    arrived = [exchange(parts[0], *moved)]
+
+    lead = pieces[0]
+    for c in range(1, col_size):
+        lead = jnp.where(my_col == c, lax.ppermute(pieces[c], "col", [(0, c)]), lead)
+    lead = [lead[0]] + [
+        lax.ppermute(lead[shift], "row", along_row(shift)) for shift in range(1, row_size)
+    ]
+    raw = lead_rows(capacity, front, lead)
+
+    raw, _ = lax.optimization_barrier((raw, arrived[0]))
+    same = [raw] + [lax.ppermute(raw, "col", across_col(k)) for k in range(2, col_size, 2)]
+    corner_half = jnp.stack([value[0] for value in same])
+    corner_other = lax.ppermute(corner_half, "col", across_col(1))
+    gathered = jnp.stack(same)
+    arrived.append(exchange(parts[1], corner_other))
+    other = lax.ppermute(gathered, "col", across_col(1))
+    raw_rows = order_rows(ids, same, other)
+    arrived.append(exchange(parts[2], arrived[1], other))
+
     meta = jnp.concatenate(
         [child_rows.reshape(1, slots), child_cols.reshape(1, slots), child_counts.reshape(1, 1)], axis=1
     )
-    meta = lax.all_gather(meta, ("row", "col"), axis=0, tiled=True)
-    own, lead = locate(row_size, col_size, capacity, slots, ids, meta)
-
+    meta, _ = lax.optimization_barrier((meta, corner_other))
+    meta = lax.all_gather(meta, "row", axis=0, tiled=True)
+    own = locate(row_size, capacity, slots, ids, meta)
+    *moved, _ = lax.optimization_barrier((*moved, corner_other))
     kids = jnp.concatenate(
         [moved[0]]
-        + [
-            lax.ppermute(moved[shift], "row", [(r, (r + shift) % row_size) for r in range(row_size)])
-            for shift in range(1, row_size)
-        ]
-    )
-
-    pieces = kids.reshape(arrivals, col_size, chunk, width)
-    lead_kids = jnp.where(my_col == 0, pieces[:, 0], 0.0)
-    for c in range(1, col_size):
-        lead_kids = lead_kids + lax.ppermute(pieces[:, c], "col", [(0, c)])
-    raw, corner = lead_rows(ids, lead, front[:, 0, :, 0, 0, :], lead_kids)
-
-    corner = lax.psum(corner, ("row", "col"))
+        + [lax.ppermute(moved[shift], "row", along_row(shift)) for shift in range(1, row_size)]
+    )
+
+    corner_mine = order_rows(
+        ids, [corner_half[k : k + 1] for k in range(col_size // 2)], corner_other[:, None]
+    ).reshape(width, width)
+    corner = corner_mine
+    corner = jnp.where(my_row == 0, corner, 0.0)
+    for shift in range(1, row_size):
+        corner = corner + lax.ppermute(corner_mine, "row", [(0, shift)])
     corner = 0.5 * (corner + corner.T)
     factor = jnp.linalg.cholesky(corner)
     inverse = jax.scipy.linalg.solve_triangular(
         factor, jnp.eye(width, dtype=jnp.float32), lower=True
     )
 
-    raw_rows = lax.all_gather(raw, "col", axis=0, tiled=False)
     mine = lax.dynamic_index_in_dim(
         raw_rows.reshape(col_size, col_tiles, group, chunk, width),
         my_col // row_size,
@@ -440,20 +538,30 @@
     )
     raw_cols = jnp.where(my_row == my_col % row_size, mine, 0.0)
     for shift in range(1, row_size):
-        pairs = [
+        steps = [
             ((c % row_size) * col_size + c, ((c + shift) % row_size) * col_size + c)
             for c in range(col_size)
         ]
-        raw_cols = raw_cols + lax.ppermute(mine, ("row", "col"), pairs)
-    rows, cols = panels(ids, inverse, factor, raw_rows, raw_cols)
-
-    later, rows, cols = lax.optimization_barrier((packed[1], rows, cols))
-    second = lax.all_to_all(later, "col", split_axis=0, concat_axis=0, tiled=True)
+        raw_cols = raw_cols + lax.ppermute(mine, ("row", "col"), steps)
+    rows, high, low = panels(ids, inverse, factor, raw_rows, raw_cols)
 
     out = None
-    for part, recv in zip(parts, (first, second)):
+    for step, part in enumerate(parts):
+        if step == 2:
+            arrived.append(exchange(parts[3], arrived[2], out))
         out = finish(
-            part, [counts[a] for a in part], row_size, col_size, ids, own, recv, rows, cols, kids, out
+            part,
+            [counts[a] for a in part],
+            row_size,
+            col_size,
+            ids,
+            own,
+            arrived[step],
+            rows,
+            high,
+            low,
+            kids,
+            out,
         )
     return out.reshape(row_tiles, 1, width, col_tiles, 1, width)
 

time: 800 us -> 577 us (0.72)
  blocking collectives: 225 us -> 20.1 us
  waiting for transfers between devices: 343 us -> 258 us
  starting transfers between devices: 28.6 us -> 82.4 us
  Pallas kernels: 89.9 us -> 116 us
  between operations: 17.7 us -> 3.04 us
    all_gather x1, blocking collectives: 225 us -> 20.1 us  [on_device(): meta = lax.all_gather(meta, 'row', axis=0, tiled=True)]
    psum x1 -> x0, waiting for transfers between devices: 151 us -> none  [on_device(): corner = lax.psum(corner, ('row', 'col'))]
    ppermute x13 -> x24, waiting for transfers between devices: 100 us -> 184 us  [the longest x1 92.5 us: on_device(): other = lax.ppermute(gathered, 'col', across_col(1))]
    ppermute x13 -> x24, starting transfers between devices: 16.7 us -> 51.8 us  [the longest x3 18.2 us: on_device(): lax.ppermute(raw, 'col', across_col(k))]
    all_to_all x2 -> x4, starting transfers between devices: 11.5 us -> 30.6 us  [exchange(): lax.all_to_all(blocks, 'col', split_axis=0, concat_axis=0, tiled=True)]
    all_to_all x2 -> x4, waiting for transfers between devices: 90.9 us -> 73.8 us  [exchange(): lax.all_to_all(blocks, 'col', split_axis=0, concat_axis=0, tiled=True)]
    pallas_call x2 -> x4, Pallas kernels: 4.3 us -> 12.8 us  [the longest x2 6.25 us: order_rows(): pl.pallas_call(order_kernel, out_shape=jax.ShapeDtypeStruct((2 * len(same...]
    pallas_call x2 -> x4, Pallas kernels: 40.6 us -> 48.2 us  [finish(): pl.pallas_call(functools.partial(finish_kernel, depths, counts, row_size,...]
  transfers between devices with their start and end apart: 17 -> 28, of which waited for: 7 -> 10; matrix products, arithmetic and copies ran while one was open for 10% -> 14% of each run, Pallas kernels for 7% -> 16%
where the time goes in v2:
time: 577 us; the launch traced here: 566 us
  waiting for transfers between devices  258 us (45%)
  Pallas kernels  116 us (20%)
  starting transfers between devices  82.4 us (14%)
  other arithmetic  66.4 us (12%)
  blocking collectives  20.1 us (3%)
  local copies, waits for them, and re-layouts  19.2 us (3%)
    ppermute x1, waiting for transfers between devices, on_device(): other = lax.ppermute(gathered, 'col', across_col(1))  92.5 us
    all_to_all x4, waiting for transfers between devices, exchange(): lax.all_to_all(blocks, 'col', split_axis=0, concat_axis=0, tiled=True)  73.8 us
    ppermute x7, waiting for transfers between devices, on_device(): lax.ppermute(pieces[c], 'col', [(0, c)])  50 us
    pallas_call x4, Pallas kernels, finish(): pl.pallas_call(functools.partial(finish_kernel, depths, counts, row_size,...  48.2 us
    ppermute x3, waiting for transfers between devices, on_device(): lax.ppermute(raw, 'col', across_col(k))  34.7 us
    another operation x6, other arithmetic, on_device(): factor = jnp.linalg.cholesky(corner)  34 us
    all_to_all x4, starting transfers between devices, exchange(): lax.all_to_all(blocks, 'col', split_axis=0, concat_axis=0, tiled=True)  30.6 us
    pallas_call x4, Pallas kernels, pack(): pl.pallas_call(functools.partial(pack_kernel, depths, counts), out_shape=...  27.4 us
  transfers between devices with their start and end apart: 28, of which 10 were waited for; matrix products, arithmetic and copies ran while one was open for 14% of the time, Pallas kernels for 16%

profile of v2, /device:TPU:6, one launch (start us, length us, event | category | flops | bytes accessed | tf_op | source)
XLA Modules:
  0.0 566.2 jit_solution(14758407530093227849)
XLA Ops:
  8.0 12.4 %move_tiles.1 = (f32[2,256,256]{2,1,0:T(8,128)}, f32[2,256,256]{2,1,0:T(8,128)}, f32[2,256,256]{2,1,0:T(8,128)}, f32[2,256,256]{2,1,0:T(8,128)}, f32[4,80,256]{2...) custom-call(s32[2]{0:T(128)} %pad_add_fusion.ids_ref, ...), custom_call_target="tpu_custom_call" | custom-call | tf_op jit(solution)/shard_map/move_tiles/pallas_call | solution.py:86
  20.4 6.5 %all-to-all-start = ((f32[8,8,32,256]{3,2,1,0:T(8,128)}), f32[8,8,32,256]{3,2,1,0:T(8,128)S(1)}, u32[]{:S(2)}, u32[]{:S(2)}) async-start(f32[8,8,32,256]{3,2,1,0:T(8,128)} %pack.4), calls=%async_computation | async-start | bytes 4194304 | tf_op jit(solution)/shard_map/all_to_all | solution.py:467
  34.5 49.9 %collective-permute-done.6 = f32[4,80,256]{2,1,0:T(8,128)} collective-permute-done((f32[4,80,256]{2,1,0:T(8,128)}, f32[4,80,256]{2,1,0:T(8,128)}, u32[]{:S(2)}, u32[]{:S(2)}) %collective-permute-start.6) | collective-permute-done | bytes 327712 | tf_op jit(solution)/shard_map/ppermute | solution.py:492
  96.8 15.8 %collective-permute-start.10 = (f32[16,32,256]{2,1,0:T(8,128)}, f32[16,32,256]{2,1,0:T(8,128)S(1)}, u32[]{:S(2)}, u32[]{:S(2)}) collective-permute-start(f32[16,32,256]{2,1,0:T(8,128)} %lead_rows.1.refs_0_), channel_id=1, source_target_pairs={{0,2},{1,3},{2,0},{3,1},{4,6},{5,7},{6,4},{7,5},{8,10},{9,11},{10,... | collective-permute-start | bytes 1572872 | tf_op jit(solution)/shard_map/ppermute | solution.py:499
  115.8 9.5 %collective-permute-done.10.refs_1_ = f32[16,32,256]{2,1,0:T(8,128)S(1)} collective-permute-done((f32[16,32,256]{2,1,0:T(8,128)}, f32[16,32,256]{2,1,0:T(8,128)S(1)}, u32[]{:S(2)}, u32[]{:S(2)}) %collective-permute-start.10) | collective-permute-done | bytes 524320 | tf_op jit(solution)/shard_map/ppermute | solution.py:499
  125.4 25.1 %collective-permute-done.11.refs_2_ = f32[16,32,256]{2,1,0:T(8,128)S(1)} collective-permute-done((f32[16,32,256]{2,1,0:T(8,128)}, f32[16,32,256]{2,1,0:T(8,128)S(1)}, u32[]{:S(2)}, u32[]{:S(2)}) %collective-permute-start.11) | collective-permute-done | bytes 524320 | tf_op jit(solution)/shard_map/ppermute | solution.py:499
  151.5 6.5 %collective-permute-start.13 = (f32[4,32,256]{2,1,0:T(8,128)S(1)}, f32[4,32,256]{2,1,0:T(8,128)S(1)}, u32[]{:S(2)}, u32[]{:S(2)}) collective-permute-start(f32[4,32,256]{2,1,0:T(8,128)S(1)} %pad_maximum_fusion.2), channel_id=1, source_target_pairs={{0,1},{1,0},{2,3},{3,2},{4,5},{5,4},{6,7},{7,6},{8,9},{9,8},{10,11... | collective-permute-start | bytes 393224 | tf_op jit(solution)/shard_map/ppermute | solution.py:501
  158.0 8.0 %pack.7 = f32[8,22,32,256]{3,2,1,0:T(8,128)} custom-call(f32[16,1,32,8,8,256]{5,4,3,2,1,0:T(8,128)} %front_ref.9), custom_call_target="tpu_custom_call" | custom-call | tf_op jit(solution)/shard_map/pack/pallas_call | solution.py:300
  166.7 14.3 %all-to-all-start.1 = ((f32[8,22,32,256]{3,2,1,0:T(8,128)}), f32[8,22,32,256]{3,2,1,0:T(8,128)}, u32[]{:S(2)}, u32[]{:S(2)}) async-start(f32[8,22,32,256]{3,2,1,0:T(8,128)} %pack.7), calls=%async_computation.1 | async-start | bytes 11534336 | tf_op jit(solution)/shard_map/all_to_all | solution.py:467
  182.7 12.6 %pack.6 = f32[8,37,32,256]{3,2,1,0:T(8,128)} custom-call(f32[16,1,32,8,8,256]{5,4,3,2,1,0:T(8,128)} %front_ref.9), custom_call_target="tpu_custom_call" | custom-call | tf_op jit(solution)/shard_map/pack/pallas_call | solution.py:300
  195.3 92.5 %collective-permute-done.14.refs_4_ = f32[4,16,32,256]{3,2,1,0:T(8,128)} collective-permute-done((f32[4,16,32,256]{3,2,1,0:T(8,128)}, f32[4,16,32,256]{3,2,1,0:T(8,128)}, u32[]{:S(2)}, u32[]{:S(2)}) %collective-permute-start.14) | collective-permute-done | bytes 2097184 | tf_op jit(solution)/shard_map/ppermute | solution.py:504
  287.8 19.7 %all-to-all-done.1.recv_ref = f32[8,22,32,256]{3,2,1,0:T(8,128)} async-done(((f32[8,22,32,256]{3,2,1,0:T(8,128)}), f32[8,22,32,256]{3,2,1,0:T(8,128)}, u32[]{:S(2)}, u32[]{:S(2)}) %all-to-all-start.1) | async-done | bytes 5767200 | tf_op jit(solution)/shard_map/all_to_all | solution.py:467
  324.4 20.1 %all-gather = s32[4,1,17]{2,1,0:T(1,128)} all-gather(s32[1,1,17]{2,1,0:T(1,128)S(1)} %bitcast.91), channel_id=1, replica_groups=mesh['row'=4,'col'=8] {'row'}, dimensions={0}, use_global_device_ids=true | all-gather | bytes 340 | tf_op jit(solution)/shard_map/all_gather | solution.py:512
  348.6 11.7 %cholesky.49 = f32[128,128]{1,0:T(8,128)S(1)} custom-call(f32[128,128]{1,0:T(8,128)S(1)} %cholesky.115), custom_call_target="Cholesky" | custom-call | tf_op jit(solution)/shard_map/jit(cholesky)/cholesky | solution.py:528
  360.4 9.8 %custom-call.15 = f32[1,128,128]{1,2,0:T(8,128)S(1)} custom-call(f32[1,128,128]{2,1,0:T(8,128)S(1)} %get-tuple-element.82), custom_call_target="InvertDiagBlocksLowerTriangular" | custom-call | tf_op jit(solution)/shard_map/jit(cholesky)/cholesky | solution.py:528
  370.6 11.7 %cholesky.103 = f32[128,128]{1,0:T(8,128)S(1)} custom-call(f32[128,128]{1,0:T(8,128)S(1)} %convolution_subtract_fusion.1), custom_call_target="Cholesky" | custom-call | tf_op jit(solution)/shard_map/jit(cholesky)/cholesky | solution.py:528
  404.0 20.5 %custom-call.16 = f32[2,128,128]{1,2,0:T(8,128)S(1)} custom-call(f32[2,128,128]{2,1,0:T(8,128)} %get-tuple-element.62), custom_call_target="InvertDiagBlocksLowerTriangular" | custom-call | tf_op jit(solution)/shard_map/jit(_solve_triangular)/triangular_solve | solution.py:529
  442.7 15.4 %panels.1 = (f32[16,256,256]{2,1,0:T(8,128)}, bf16[8,256,256]{2,1,0:T(8,128)(2,1)}, bf16[8,256,256]{2,1,0:T(8,128)(2,1)}) custom-call(s32[2]{0:T(128)} %pad_add_fusion.ids_ref, f32[256,256]{1,0:T(8,128)} %pad_maximum_fusion.1.inverse_ref, f32[256,256]{1,0:T(8,128)} %get-tuple-element.72.factor_ref, f32[8,16,32,256]{3,2,1,0:T(8,128)} %order_rows.3.rows_ref, ...), custom_call_target="tpu_custom_call" | custom-call | tf_op jit(solution)/shard_map/panels/pallas_call | solution.py:237
  458.0 6.8 %finish.4.rest_0_ = f32[16,4096,128]{2,1,0:T(8,128)} custom-call(s32[2]{0:T(128)} %pad_add_fusion.ids_ref, s32[2,8]{1,0:T(2,128)} %locate.1.own_ref, f32[8,8,32,256]{3,2,1,0:T(8,128)} %copy-done.2, f32[16,256,256]{2,1,0:T(8,128)} %get-tuple-element.47.rows_ref, bf16[8,256,256]{2,1,0:T(8,128)(2,1)} %get-tuple-element.48.high_ref, ...), custom_call_target="tpu_custom_call" | custom-call | tf_op jit(solution)/shard_map/finish/pallas_call | solution.py:429
  464.9 11.1 %finish.5.rest_0_ = f32[16,4096,128]{2,1,0:T(8,128)} custom-call(s32[2]{0:T(128)} %pad_add_fusion.ids_ref, s32[2,8]{1,0:T(2,128)} %locate.1.own_ref, f32[8,22,32,256]{3,2,1,0:T(8,128)} %all-to-all-done.1.recv_ref, f32[16,256,256]{2,1,0:T(8,128)} %get-tuple-element.47.rows_ref, ...), custom_call_target="tpu_custom_call", output_to_operand_aliasing={{}: (7, {})} | custom-call | tf_op jit(solution)/shard_map/finish/pallas_call | solution.py:429
  475.9 46.9 %all-to-all-done.2.recv_ref = f32[8,37,32,256]{3,2,1,0:T(8,128)} async-done(((f32[8,37,32,256]{3,2,1,0:T(8,128)}), f32[8,37,32,256]{3,2,1,0:T(8,128)}, u32[]{:S(2)}, u32[]{:S(2)}) %all-to-all-start.2) | async-done | bytes 9699360 | tf_op jit(solution)/shard_map/all_to_all | solution.py:467
  527.1 23.8 %finish.6.rest_0_ = f32[16,4096,128]{2,1,0:T(8,128)} custom-call(s32[2]{0:T(128)} %pad_add_fusion.ids_ref, s32[2,8]{1,0:T(2,128)} %locate.1.own_ref, f32[8,37,32,256]{3,2,1,0:T(8,128)} %all-to-all-done.2.recv_ref, f32[16,256,256]{2,1,0:T(8,128)} %get-tuple-element.47.rows_ref, ...), custom_call_target="tpu_custom_call", output_to_operand_aliasing={{}: (7, {})} | custom-call | tf_op jit(solution)/shard_map/finish/pallas_call | solution.py:429
  550.9 7.2 %all-to-all-done.3.recv_ref = f32[8,5,32,256]{3,2,1,0:T(8,128)S(1)} async-done(((f32[8,5,32,256]{3,2,1,0:T(8,128)}), f32[8,5,32,256]{3,2,1,0:T(8,128)S(1)}, u32[]{:S(2)}, u32[]{:S(2)}) %all-to-all-start.3) | async-done | bytes 1310752 | tf_op jit(solution)/shard_map/all_to_all | solution.py:467
  559.1 6.6 %finish.7 = f32[16,4096,128]{2,1,0:T(8,128)} custom-call(s32[2]{0:T(128)} %pad_add_fusion.ids_ref, s32[2,8]{1,0:T(2,128)} %locate.1.own_ref, f32[8,5,32,256]{3,2,1,0:T(8,128)} %copy-done.3, f32[16,256,256]{2,1,0:T(8,128)} %get-tuple-element.47.rows_ref, bf16[8,256,256]{2,1,0:T(8,128)(2,1)} %get-tuple-element.48.high_ref, ...), custom_call_target="tpu_custom_call", output_to_operand_aliasing={{}: (7, {})} | custom-call | tf_op jit(solution)/shard_map/finish/pallas_call | solution.py:429
  (147 shorter events, 104.2 us)
Async XLA Ops:
  20.4 76.4 %all-to-all-start = ((f32[8,8,32,256]{3,2,1,0:T(8,128)}), f32[8,8,32,256]{3,2,1,0:T(8,128)S(1)}, u32[]{:S(2)}, u32[]{:S(2)}) async-start(f32[8,8,32,256]{3,2,1,0:T(8,128)} %pack.4), calls=%async_computation | async-start | bytes 4194304 | tf_op jit(solution)/shard_map/all_to_all | solution.py:467
  26.9 4.9 collective-permute-start
  27.5 5.6 collective-permute-start.1
  28.2 6.2 %collective-permute-start.2 = (f32[4,80,256]{2,1,0:T(8,128)}, f32[4,80,256]{2,1,0:T(8,128)S(1)}, u32[]{:S(2)}, u32[]{:S(2)}) collective-permute-start(f32[4,80,256]{2,1,0:T(8,128)} %get-tuple-element.32), channel_id=1, source_target_pairs={{0,5},{8,13},{16,21},{24,29}} | collective-permute-start | bytes 983048 | tf_op jit(solution)/shard_map/ppermute | solution.py:492
  28.9 5.5 collective-permute-start.3
  33.1 51.3 %collective-permute-start.6 = (f32[4,80,256]{2,1,0:T(8,128)}, f32[4,80,256]{2,1,0:T(8,128)}, u32[]{:S(2)}, u32[]{:S(2)}) collective-permute-start(f32[4,80,256]{2,1,0:T(8,128)} %get-tuple-element.36), channel_id=1, source_target_pairs={{0,1},{8,9},{16,17},{24,25}} | collective-permute-start | bytes 983048 | tf_op jit(solution)/shard_map/ppermute | solution.py:492
  86.2 5.3 collective-permute-start.8
  96.8 28.6 %collective-permute-start.10 = (f32[16,32,256]{2,1,0:T(8,128)}, f32[16,32,256]{2,1,0:T(8,128)S(1)}, u32[]{:S(2)}, u32[]{:S(2)}) collective-permute-start(f32[16,32,256]{2,1,0:T(8,128)} %lead_rows.1.refs_0_), channel_id=1, source_target_pairs={{0,2},{1,3},{2,0},{3,1},{4,6},{5,7},{6,4},{7,5},{8,10},{9,11},{10,... | collective-permute-start | bytes 1572872 | tf_op jit(solution)/shard_map/ppermute | solution.py:499
  112.6 37.9 %collective-permute-start.11 = (f32[16,32,256]{2,1,0:T(8,128)}, f32[16,32,256]{2,1,0:T(8,128)S(1)}, u32[]{:S(2)}, u32[]{:S(2)}) collective-permute-start(f32[16,32,256]{2,1,0:T(8,128)} %lead_rows.1.refs_0_), channel_id=1, source_target_pairs={{0,4},{1,5},{2,6},{3,7},{4,0},{5,1},{6,2},{7,3},{8,12},{9,13},{10,... | collective-permute-start | bytes 1572872 | tf_op jit(solution)/shard_map/ppermute | solution.py:499
  112.6 37.9 %collective-permute-start.12 = (f32[16,32,256]{2,1,0:T(8,128)}, f32[16,32,256]{2,1,0:T(8,128)S(1)}, u32[]{:S(2)}, u32[]{:S(2)}) collective-permute-start(f32[16,32,256]{2,1,0:T(8,128)} %lead_rows.1.refs_0_), channel_id=1, source_target_pairs={{0,6},{1,7},{2,4},{3,5},{4,2},{5,3},{6,0},{7,1},{8,14},{9,15},{10,... | collective-permute-start | bytes 1572872 | tf_op jit(solution)/shard_map/ppermute | solution.py:499
  151.5 14.6 %collective-permute-start.13 = (f32[4,32,256]{2,1,0:T(8,128)S(1)}, f32[4,32,256]{2,1,0:T(8,128)S(1)}, u32[]{:S(2)}, u32[]{:S(2)}) collective-permute-start(f32[4,32,256]{2,1,0:T(8,128)S(1)} %pad_maximum_fusion.2), channel_id=1, source_target_pairs={{0,1},{1,0},{2,3},{3,2},{4,5},{5,4},{6,7},{7,6},{8,9},{9,8},{10,11... | collective-permute-start | bytes 393224 | tf_op jit(solution)/shard_map/ppermute | solution.py:501
  166.7 140.7 %all-to-all-start.1 = ((f32[8,22,32,256]{3,2,1,0:T(8,128)}), f32[8,22,32,256]{3,2,1,0:T(8,128)}, u32[]{:S(2)}, u32[]{:S(2)}) async-start(f32[8,22,32,256]{3,2,1,0:T(8,128)} %pack.7), calls=%async_computation.1 | async-start | bytes 11534336 | tf_op jit(solution)/shard_map/all_to_all | solution.py:467
  182.7 105.1 %collective-permute-start.14 = (f32[4,16,32,256]{3,2,1,0:T(8,128)}, f32[4,16,32,256]{3,2,1,0:T(8,128)}, u32[]{:S(2)}, u32[]{:S(2)}) collective-permute-start(f32[4,16,32,256]{3,2,1,0:T(8,128)} %pad_maximum_fusion), channel_id=1, source_target_pairs={{0,1},{1,0},{2,3},{3,2},{4,5},{5,4},{6,7},{7,6},{8,9},{9,8},{10,11... | collective-permute-start | bytes 6291464 | tf_op jit(solution)/shard_map/ppermute | solution.py:504
  307.5 215.4 %all-to-all-start.2 = ((f32[8,37,32,256]{3,2,1,0:T(8,128)}), f32[8,37,32,256]{3,2,1,0:T(8,128)}, u32[]{:S(2)}, u32[]{:S(2)}) async-start(f32[8,37,32,256]{3,2,1,0:T(8,128)} %pack.6), calls=%async_computation.2 | async-start | bytes 19398656 | tf_op jit(solution)/shard_map/all_to_all | solution.py:467
  314.7 31.7 %collective-permute-start.15 = (f32[256,256]{1,0:T(8,128)}, f32[256,256]{1,0:T(8,128)S(1)}, u32[]{:S(2)}, u32[]{:S(2)}) collective-permute-start(f32[256,256]{1,0:T(8,128)} %bitcast.82), channel_id=1, source_target_pairs={{0,8},{1,9},{2,10},{3,11},{4,12},{5,13},{6,14},{7,15}} | collective-permute-start | bytes 786440 | tf_op jit(solution)/shard_map/ppermute | solution.py:526
  315.4 31.0 %collective-permute-start.16 = (f32[256,256]{1,0:T(8,128)}, f32[256,256]{1,0:T(8,128)S(1)}, u32[]{:S(2)}, u32[]{:S(2)}) collective-permute-start(f32[256,256]{1,0:T(8,128)} %bitcast.83), channel_id=1, source_target_pairs={{0,16},{1,17},{2,18},{3,19},{4,20},{5,21},{6,22},{7,23}} | collective-permute-start | bytes 786440 | tf_op jit(solution)/shard_map/ppermute | solution.py:526
  316.7 30.4 %collective-permute-start.17 = (f32[256,256]{1,0:T(8,128)}, f32[256,256]{1,0:T(8,128)}, u32[]{:S(2)}, u32[]{:S(2)}) collective-permute-start(f32[256,256]{1,0:T(8,128)} %bitcast.84), channel_id=1, source_target_pairs={{0,24},{1,25},{2,26},{3,27},{4,28},{5,29},{6,30},{7,31}} | collective-permute-start | bytes 786440 | tf_op jit(solution)/shard_map/ppermute | solution.py:526
  320.9 104.1 %collective-permute-start.21 = (f32[2,256,256]{2,1,0:T(8,128)}, f32[2,256,256]{2,1,0:T(8,128)}, u32[]{:S(2)}, u32[]{:S(2)}) collective-permute-start(f32[2,256,256]{2,1,0:T(8,128)} %get-tuple-element.51), channel_id=1, source_target_pairs={{0,8},{8,16},{16,24},{24,0},{1,9},{9,17},{17,25},{25,1},{2,10},{10... | collective-permute-start | bytes 1572872 | tf_op jit(solution)/shard_map/ppermute | solution.py:517
  321.0 111.1 %collective-permute-start.22 = (f32[2,256,256]{2,1,0:T(8,128)}, f32[2,256,256]{2,1,0:T(8,128)}, u32[]{:S(2)}, u32[]{:S(2)}) collective-permute-start(f32[2,256,256]{2,1,0:T(8,128)} %get-tuple-element.52), channel_id=1, source_target_pairs={{0,16},{8,24},{16,0},{24,8},{1,17},{9,25},{17,1},{25,9},{2,18},{10... | collective-permute-start | bytes 1572872 | tf_op jit(solution)/shard_map/ppermute | solution.py:517
  392.1 44.6 %collective-permute-start.18 = (f32[8,8,32,256]{3,2,1,0:T(8,128)}, f32[8,8,32,256]{3,2,1,0:T(8,128)}, u32[]{:S(2)}, u32[]{:S(2)}) collective-permute-start(f32[8,8,32,256]{3,2,1,0:T(8,128)} %dynamic-slice_bitcast_fusion), channel_id=1, source_target_pairs={{0,8},{9,17},{18,26},{27,3},{4,12},{13,21},{22,30},{31,7}} | collective-permute-start | bytes 6291464 | tf_op jit(solution)/shard_map/ppermute | solution.py:545
  393.5 43.2 %collective-permute-start.19 = (f32[8,8,32,256]{3,2,1,0:T(8,128)}, f32[8,8,32,256]{3,2,1,0:T(8,128)}, u32[]{:S(2)}, u32[]{:S(2)}) collective-permute-start(f32[8,8,32,256]{3,2,1,0:T(8,128)} %dynamic-slice_bitcast_fusion), channel_id=1, source_target_pairs={{0,16},{9,25},{18,2},{27,11},{4,20},{13,29},{22,6},{31,15}} | collective-permute-start | bytes 6291464 | tf_op jit(solution)/shard_map/ppermute | solution.py:545
  395.6 41.1 %collective-permute-start.20 = (f32[8,8,32,256]{3,2,1,0:T(8,128)}, f32[8,8,32,256]{3,2,1,0:T(8,128)}, u32[]{:S(2)}, u32[]{:S(2)}) collective-permute-start(f32[8,8,32,256]{3,2,1,0:T(8,128)} %dynamic-slice_bitcast_fusion), channel_id=1, source_target_pairs={{0,24},{9,1},{18,10},{27,19},{4,28},{13,5},{22,14},{31,23}} | collective-permute-start | bytes 6291464 | tf_op jit(solution)/shard_map/ppermute | solution.py:545
  425.0 11.7 %collective-permute-start.23 = (f32[2,256,256]{2,1,0:T(8,128)S(1)}, f32[2,256,256]{2,1,0:T(8,128)S(1)}, u32[]{:S(2)}, u32[]{:S(2)}) collective-permute-start(f32[2,256,256]{2,1,0:T(8,128)S(1)} %copy-done.24), channel_id=1, source_target_pairs={{0,24},{8,0},{16,8},{24,16},{1,25},{9,1},{17,9},{25,17},{2,26},{10... | collective-permute-start | bytes 1572872 | tf_op jit(solution)/shard_map/ppermute | solution.py:517
  522.8 35.2 %all-to-all-start.3 = ((f32[8,5,32,256]{3,2,1,0:T(8,128)}), f32[8,5,32,256]{3,2,1,0:T(8,128)S(1)}, u32[]{:S(2)}, u32[]{:S(2)}) async-start(f32[8,5,32,256]{3,2,1,0:T(8,128)} %pack.5), calls=%async_computation.3 | async-start | bytes 2621440 | tf_op jit(solution)/shard_map/all_to_all | solution.py:467
  (29 other events, 737.5 us)

commit v3 on v2

--- a/solution.py
+++ b/solution.py
@@ -30,6 +30,10 @@
 
 def depth_blocks(a, row_size, col_size):
     return (a * row_size + row_size - 1) // col_size + 1
+
+
+def shared_blocks(a, row_size, col_size):
+    return (a * row_size + row_size - 1 - col_size // 2) // col_size + 1
 
 
 def move_kernel(
@@ -46,7 +50,7 @@
 ):
     slots, width = tiles_ref.shape[0], tiles_ref.shape[1]
     out_refs, lead_refs = out_refs[:row_size], out_refs[row_size:]
-    chunk = width // len(lead_refs)
+    chunk = width // (2 * len(lead_refs))
     labels = lax.broadcasted_iota(jnp.int32, (width, width), 0)
     count = count_ref[0]
 
@@ -59,20 +63,25 @@
             return chosen, seen + hit.astype(jnp.int32)
 
         chosen, seen = lax.fori_loop(0, slots, scan, (jnp.int32(0), jnp.int32(0)))
-        row_hot = (labels == row_map_ref[chosen]).astype(jnp.float32)
-        col_hot = (labels == col_map_ref[chosen]).astype(jnp.float32)
-        shifted = jnp.dot(
-            row_hot, tiles_ref[chosen], precision=HIGHEST, preferred_element_type=jnp.float32
-        )
-        tile = dot_nt(shifted, col_hot)
+        row_hot = (labels == row_map_ref[pl.ds(chosen, 1), :]).astype(jnp.bfloat16)
+        col_hot = (labels == col_map_ref[pl.ds(chosen, 1), :]).astype(jnp.bfloat16)
+        left = tiles_ref[chosen]
+        tile = None
+        for _ in range(3):
+            term = left.astype(jnp.bfloat16)
+            left = left - term.astype(jnp.float32)
+            moved = jnp.dot(row_hot, term, preferred_element_type=jnp.float32)
+            moved = bf16_nt(moved.astype(jnp.bfloat16), col_hot)
+            tile = moved if tile is None else tile + moved
         out_ref[place] = tile
         here = (seen > place) & (cols_ref[chosen] == 0)
         target = jnp.where(here, rows_ref[chosen] // row_size, -1).astype(jnp.float32)
-        for c, lead_ref in enumerate(lead_refs):
-            lead_ref[shift, pl.ds(place * chunk, chunk), :] = tile[c * chunk : (c + 1) * chunk]
-            lead_ref[shift, pl.ds(capacity * chunk + place * 8, 8), :] = jnp.full(
-                (8, width), target
-            )
+        mark = jnp.full((8, width), target)
+        for pair, lead_ref in enumerate(lead_refs):
+            for side in range(2):
+                first = (2 * pair + side) * chunk
+                lead_ref[side, shift, pl.ds(place * chunk, chunk), :] = tile[first : first + chunk]
+                lead_ref[side, shift, pl.ds(capacity * chunk + place * 8, 8), :] = mark
 
     for shift, out_ref in enumerate(out_refs):
         for place in range(capacity):
@@ -87,14 +96,16 @@
         functools.partial(move_kernel, row_size, capacity),
         out_shape=[jax.ShapeDtypeStruct((capacity, width, width), jnp.float32)] * row_size
         + [
-            jax.ShapeDtypeStruct((row_size, capacity * (width // col_size + 8), width), jnp.float32)
+            jax.ShapeDtypeStruct(
+                (2, row_size, capacity * (width // col_size + 8), width), jnp.float32
+            )
         ]
-        * col_size,
+        * (col_size // 2),
         in_specs=[smem, smem, smem, smem, vmem, vmem, vmem],
-        out_specs=[vmem] * (row_size + col_size),
+        out_specs=[vmem] * (row_size + col_size // 2),
         compiler_params=pltpu.CompilerParams(vmem_limit_bytes=VMEM_LIMIT),
         name="move_tiles",
-    )(ids, rows, cols, count, tiles, row_maps.reshape(slots, 1, width), col_maps.reshape(slots, 1, width))
+    )(ids, rows, cols, count, tiles, row_maps, col_maps)
 
 
 def locate_kernel(row_size, capacity, slots, ids_ref, meta_ref, own_ref):
@@ -139,8 +150,7 @@
     )(ids, meta)
 
 
-def lead_kernel(capacity, front_ref, *refs):
-    kids_refs, (out_ref, buf, sem) = refs[:-3], refs[-3:]
+def first_kernel(front_ref, out_ref, buf, sem):
     row_tiles, chunk, col_size = front_ref.shape[0], front_ref.shape[2], front_ref.shape[4]
     copies = [
         pltpu.make_async_copy(
@@ -158,29 +168,51 @@
             out_ref[a, :, half * LANES : (half + 1) * LANES] = flat[
                 pl.ds(a * chunk * col_size, chunk, stride=col_size), :
             ]
-    for kids_ref in kids_refs:
-        for place in range(capacity):
-            kid = kids_ref[pl.ds(place * chunk, chunk), :]
-            target = kids_ref[pl.ds(capacity * chunk + place * 8, 1), :]
-            for a in range(row_tiles):
-                out_ref[a] += jnp.where(target == a, kid, 0.0)
-
-
-def lead_rows(capacity, front, kids):
-    vmem = pl.BlockSpec(memory_space=pltpu.VMEM)
+
+
+def first_rows(front):
     row_tiles, chunk, col_size, width = front.shape[0], front.shape[2], front.shape[4], front.shape[5]
     return pl.pallas_call(
-        functools.partial(lead_kernel, capacity),
+        first_kernel,
         out_shape=jax.ShapeDtypeStruct((row_tiles, chunk, width), jnp.float32),
-        in_specs=[pl.BlockSpec(memory_space=pltpu.HBM)] + [vmem] * len(kids),
-        out_specs=vmem,
+        in_specs=[pl.BlockSpec(memory_space=pltpu.HBM)],
+        out_specs=pl.BlockSpec(memory_space=pltpu.VMEM),
         scratch_shapes=[
             pltpu.VMEM((2, row_tiles, chunk, col_size, LANES), jnp.float32),
             pltpu.SemaphoreType.DMA((2,)),
         ],
         compiler_params=pltpu.CompilerParams(vmem_limit_bytes=VMEM_LIMIT),
+        name="first_rows",
+    )(front)
+
+
+def lead_kernel(capacity, own_ref, *refs):
+    kids_refs, out_ref = refs[:-1], refs[-1]
+    chunk = own_ref.shape[1]
+
+    def one(a, carry):
+        total = own_ref[a]
+        for kids_ref in kids_refs:
+            for place in range(capacity):
+                kid = kids_ref[pl.ds(place * chunk, chunk), :]
+                target = kids_ref[pl.ds(capacity * chunk + place * 8, 1), :]
+                total += jnp.where(target == a.astype(jnp.float32), kid, 0.0)
+        out_ref[a] = total
+        return carry
+
+    lax.fori_loop(0, own_ref.shape[0], one, 0)
+
+
+def lead_rows(capacity, own, kids):
+    vmem = pl.BlockSpec(memory_space=pltpu.VMEM)
+    return pl.pallas_call(
+        functools.partial(lead_kernel, capacity),
+        out_shape=jax.ShapeDtypeStruct(own.shape, jnp.float32),
+        in_specs=[vmem] * (1 + len(kids)),
+        out_specs=vmem,
+        compiler_params=pltpu.CompilerParams(vmem_limit_bytes=VMEM_LIMIT),
         name="lead_rows",
-    )(front, *kids)
+    )(own, *kids)
 
 
 def order_kernel(ids_ref, *refs):
@@ -313,9 +345,50 @@
     )(front)
 
 
+def edge_kernel(blocks, ids_ref, front_ref, *refs):
+    out_refs, (buf, sem) = refs[:-2], refs[-2:]
+    chunk, col_size = front_ref.shape[2], front_ref.shape[4]
+    copies = [
+        pltpu.make_async_copy(
+            front_ref.at[a, 0, :, b, :, pl.ds(half * LANES, LANES)], buf.at[i, half], sem.at[i, half]
+        )
+        for i, (a, b) in enumerate(blocks)
+        for half in range(2)
+    ]
+    for copy in copies:
+        copy.start()
+    for copy in copies:
+        copy.wait()
+    for i in range(len(blocks)):
+        for half in range(2):
+            flat = buf.at[i, half].reshape(chunk * col_size, LANES)
+            for k, out_ref in enumerate(out_refs):
+                out_ref[i, :, half * LANES : (half + 1) * LANES] = flat[
+                    pl.ds(lax.bitwise_xor(ids_ref[1], k), chunk, stride=col_size), :
+                ]
+
+
+def pack_edge(ids, front, blocks):
+    chunk, col_size, width = front.shape[2], front.shape[4], front.shape[5]
+    vmem = pl.BlockSpec(memory_space=pltpu.VMEM)
+    return pl.pallas_call(
+        functools.partial(edge_kernel, blocks),
+        out_shape=[jax.ShapeDtypeStruct((len(blocks), chunk, width), jnp.float32)] * col_size,
+        in_specs=[pl.BlockSpec(memory_space=pltpu.SMEM), pl.BlockSpec(memory_space=pltpu.HBM)],
+        out_specs=[vmem] * col_size,
+        scratch_shapes=[
+            pltpu.VMEM((len(blocks), 2, chunk, col_size, LANES), jnp.float32),
+            pltpu.SemaphoreType.DMA((len(blocks), 2)),
+        ],
+        compiler_params=pltpu.CompilerParams(vmem_limit_bytes=VMEM_LIMIT),
+        name="pack_edge",
+    )(ids, front)
+
+
 def finish_kernel(
     depths,
-    counts,
+    shared,
+    edges,
     row_size,
     col_size,
     ids_ref,
@@ -327,7 +400,9 @@
     kids_ref,
     *rest,
 ):
-    out_ref, in_buf, row_buf, out_buf, in_sem, row_sem, out_sem = rest[-7:]
+    edge_refs = rest[:col_size]
+    out_ref, in_buf, row_buf, out_buf, high_buf, low_buf, kid_buf, *sems = rest[-13:]
+    in_sem, row_sem, out_sem, col_sem, kid_sem, edge_sem = sems
     my_row, my_col = ids_ref[0], ids_ref[1]
     width = high_ref.shape[1]
     chunk = width // col_size
@@ -335,20 +410,40 @@
     blocks = high_ref.shape[0]
     stride = blocks * halves
 
+    counts = [n + (edge is not None) for n, edge in zip(shared, edges)]
+
     def fetch(i):
-        a, nb, slot, first = depths[i], counts[i], i % 2, sum(counts[:i])
-        return (
-            pltpu.make_async_copy(
-                recv_ref.at[:, pl.ds(first, nb)], in_buf.at[slot, :, pl.ds(0, nb)], in_sem.at[slot]
-            ),
-            pltpu.make_async_copy(rows_ref.at[a], row_buf.at[slot], row_sem.at[slot]),
-        )
+        a, nb, edge, slot, first = depths[i], shared[i], edges[i], i % 2, sum(shared[:i])
+        copies = [pltpu.make_async_copy(rows_ref.at[a], row_buf.at[slot], row_sem.at[slot])]
+        if nb:
+            copies.append(
+                pltpu.make_async_copy(
+                    recv_ref.at[:, pl.ds(first, nb)],
+                    in_buf.at[slot, :, pl.ds(0, nb)],
+                    in_sem.at[slot],
+                )
+            )
+        if edge is not None:
+            for k, edge_ref in enumerate(edge_refs):
+                copies.append(
+                    pltpu.make_async_copy(
+                        edge_ref.at[edge],
+                        in_buf.at[slot, lax.bitwise_xor(my_col, k), nb],
+                        edge_sem.at[slot, k],
+                    )
+                )
+        return copies
 
     def send(i):
         return pltpu.make_async_copy(out_buf.at[i % 2], out_ref.at[depths[i]], out_sem.at[i % 2])
 
+    most = high_buf.shape[0]
+    columns = [
+        pltpu.make_async_copy(high_ref.at[pl.ds(0, most)], high_buf, col_sem.at[0]),
+        pltpu.make_async_copy(low_ref.at[pl.ds(0, most)], low_buf, col_sem.at[1]),
+    ]
     steps = len(depths)
-    for copy in fetch(0):
+    for copy in (*fetch(0), *columns):
         copy.start()
     for i in range(steps):
         a, nb, slot = depths[i], counts[i], i % 2
@@ -357,14 +452,19 @@
                 copy.start()
         for copy in fetch(i):
             copy.wait()
+        if i == 0:
+            for copy in columns:
+                copy.wait()
         if i >= 2:
             send(i - 2).wait()
         for n in range(kids_ref.shape[0]):
 
             @pl.when(own_ref[0, n] == a)
             def _():
-                b = own_ref[1, n]
-                in_buf[slot, :, b] += kids_ref[n].reshape(col_size, chunk, width)
+                copy = pltpu.make_async_copy(kids_ref.at[n], kid_buf, kid_sem)
+                copy.start()
+                copy.wait()
+                in_buf[slot, :, own_ref[1, n]] += kid_buf[...].reshape(col_size, chunk, width)
 
         tile_i = a * row_size + my_row
 
@@ -377,8 +477,8 @@
         row_high, row_low = halves_of(row_buf[slot])
 
         def update(b):
-            return bf16_nt(row_high, high_ref[b]) + (
-                bf16_nt(row_high, low_ref[b]) + bf16_nt(row_low, high_ref[b])
+            return bf16_nt(row_high, high_buf[b]) + (
+                bf16_nt(row_high, low_buf[b]) + bf16_nt(row_low, high_buf[b])
             )
 
         for b in range(nb):
@@ -412,22 +512,24 @@
         send(i).wait()
 
 
-def finish(depths, counts, row_size, col_size, ids, own, recv, rows, high, low, kids, out=None):
+def finish(
+    depths, shared, edges, row_size, col_size, ids, own, recv, rows, high, low, kids, edge, out=None
+):
     smem = pl.BlockSpec(memory_space=pltpu.SMEM)
-    vmem = pl.BlockSpec(memory_space=pltpu.VMEM)
     hbm = pl.BlockSpec(memory_space=pltpu.HBM)
     blocks, width = high.shape[0], high.shape[1]
     chunk = width // col_size
     lines = width * blocks * (width // LANES)
-    operands = [ids, own, recv, rows, high, low, kids]
-    in_specs = [smem, smem, hbm, hbm, vmem, vmem, vmem]
+    counts = [n + (edge is not None) for n, edge in zip(shared, edges)]
+    operands = [ids, own, recv, rows, high, low, kids, *edge]
+    in_specs = [smem, smem] + [hbm] * (5 + len(edge))
     aliases = {}
     if out is not None:
         operands.append(out)
         in_specs.append(hbm)
-        aliases = {7: 0}
-    return pl.pallas_call(
-        functools.partial(finish_kernel, depths, counts, row_size, col_size),
+        aliases = {len(operands) - 1: 0}
+    return pl.pallas_call(
+        functools.partial(finish_kernel, depths, shared, edges, row_size, col_size),
         out_shape=jax.ShapeDtypeStruct((rows.shape[0], lines, LANES), jnp.float32),
         in_specs=in_specs,
         out_specs=hbm,
@@ -435,9 +537,15 @@
             pltpu.VMEM((2, col_size, max(counts), chunk, width), jnp.float32),
             pltpu.VMEM((2, width, width), jnp.float32),
             pltpu.VMEM((2, lines, LANES), jnp.float32),
+            pltpu.VMEM((max(counts), width, width), jnp.bfloat16),
+            pltpu.VMEM((max(counts), width, width), jnp.bfloat16),
+            pltpu.VMEM((width, width), jnp.float32),
             pltpu.SemaphoreType.DMA((2,)),
             pltpu.SemaphoreType.DMA((2,)),
             pltpu.SemaphoreType.DMA((2,)),
+            pltpu.SemaphoreType.DMA((2,)),
+            pltpu.SemaphoreType.DMA,
+            pltpu.SemaphoreType.DMA((2, col_size)),
         ],
         input_output_aliases=aliases,
         compiler_params=pltpu.CompilerParams(vmem_limit_bytes=VMEM_LIMIT),
@@ -455,14 +563,22 @@
     group = col_size // row_size
     ids = jnp.stack([my_row, my_col]).astype(jnp.int32)
 
-    counts = [depth_blocks(a, row_size, col_size) for a in range(row_tiles)]
+    shared = [shared_blocks(a, row_size, col_size) for a in range(row_tiles)]
+    edge_blocks = [
+        (a, shared[a]) for a in range(row_tiles) if depth_blocks(a, row_size, col_size) > shared[a]
+    ]
+    edge_of = {a: i for i, (a, _) in enumerate(edge_blocks)}
+    last = (row_tiles - 5) * 3 // 4 + 1
     parts = [[row_tiles - 2], [row_tiles - 1, row_tiles - 3, row_tiles - 4]]
-    last = (row_tiles - 5) * 3 // 4
     parts.append([a for a in range(row_tiles - 5, -1, -1) if a != last])
     parts.append([last])
 
-    def exchange(part, *after):
-        blocks = pack(front, part, [counts[a] for a in part])
+    def packed(part, *after):
+        held = lax.optimization_barrier((front,) + after)[0]
+        sent = [a for a in part if shared[a]]
+        return pack(held, sent, [shared[a] for a in sent])
+
+    def exchange(blocks, *after):
         blocks = lax.optimization_barrier((blocks,) + after)[0]
         return lax.all_to_all(blocks, "col", split_axis=0, concat_axis=0, tiled=True)
 
@@ -485,42 +601,57 @@
         col_maps.reshape(slots, width),
     )
     moved, pieces = moved[:row_size], moved[row_size:]
-    arrived = [exchange(parts[0], *moved)]
-
-    lead = pieces[0]
-    for c in range(1, col_size):
-        lead = jnp.where(my_col == c, lax.ppermute(pieces[c], "col", [(0, c)]), lead)
+
+    sent = [
+        lax.ppermute(pieces[pair], "col", [(0, 2 * pair)]) for pair in range(1, col_size // 2)
+    ]
+    edge = pack_edge(ids, lax.optimization_barrier((front, pieces[0]))[0], edge_blocks)
+
+    def send_edge(k, value):
+        steps = [
+            (r * col_size + c, r * col_size + (c ^ k))
+            for r in range(row_size)
+            for c in range(col_size)
+            if c ^ k <= r
+        ]
+        return lax.ppermute(value, ("row", "col"), steps)
+
+    half = col_size // 2
+    far = [send_edge(k, edge[k]) for k in range(half, col_size)]
+    second = packed(parts[1], pieces[0])
+    blocks = packed(parts[0], pieces[0])
+    first = first_rows(front)
+    meta = jnp.concatenate(
+        [child_rows.reshape(1, slots), child_cols.reshape(1, slots), child_counts.reshape(1, 1)], axis=1
+    )
+    meta, _ = lax.optimization_barrier((meta, pieces[0]))
+    meta = lax.all_gather(meta, "row", axis=0, tiled=True)
+    own = locate(row_size, capacity, slots, ids, meta)
+    *sent, second, first, own = lax.optimization_barrier((*sent, second, first, own))
+    arrived = [exchange(blocks, *sent, *far)]
+    lead = jnp.where(my_col == 0, pieces[0], sum(sent[1:], sent[0]))
+    other = lax.ppermute(lead[1], "col", [(c, c + 1) for c in range(0, col_size, 2)])
+    lead = jnp.where(my_col % 2 == 0, lead[0], other)
     lead = [lead[0]] + [
         lax.ppermute(lead[shift], "row", along_row(shift)) for shift in range(1, row_size)
     ]
-    raw = lead_rows(capacity, front, lead)
-
-    raw, _ = lax.optimization_barrier((raw, arrived[0]))
+    raw = lead_rows(capacity, first, lead)
+
     same = [raw] + [lax.ppermute(raw, "col", across_col(k)) for k in range(2, col_size, 2)]
-    corner_half = jnp.stack([value[0] for value in same])
-    corner_other = lax.ppermute(corner_half, "col", across_col(1))
-    gathered = jnp.stack(same)
-    arrived.append(exchange(parts[1], corner_other))
-    other = lax.ppermute(gathered, "col", across_col(1))
+    near = [send_edge(k, lax.optimization_barrier((edge[k], raw))[0]) for k in range(1, half)]
+    arrived.append(exchange(second, arrived[0], *same, *near))
+    other = lax.ppermute(jnp.stack(same), "col", across_col(1))
     raw_rows = order_rows(ids, same, other)
-    arrived.append(exchange(parts[2], arrived[1], other))
-
-    meta = jnp.concatenate(
-        [child_rows.reshape(1, slots), child_cols.reshape(1, slots), child_counts.reshape(1, 1)], axis=1
-    )
-    meta, _ = lax.optimization_barrier((meta, corner_other))
-    meta = lax.all_gather(meta, "row", axis=0, tiled=True)
-    own = locate(row_size, capacity, slots, ids, meta)
-    *moved, _ = lax.optimization_barrier((*moved, corner_other))
+    arrived.append(exchange(packed(parts[2], same[1]), arrived[1], other))
+    edge = [edge[0], *near, *far]
+
+    *moved, _ = lax.optimization_barrier((*moved, raw))
     kids = jnp.concatenate(
         [moved[0]]
         + [lax.ppermute(moved[shift], "row", along_row(shift)) for shift in range(1, row_size)]
     )
 
-    corner_mine = order_rows(
-        ids, [corner_half[k : k + 1] for k in range(col_size // 2)], corner_other[:, None]
-    ).reshape(width, width)
-    corner = corner_mine
+    corner_mine = corner = raw_rows[:, 0].reshape(width, width)
     corner = jnp.where(my_row == 0, corner, 0.0)
     for shift in range(1, row_size):
         corner = corner + lax.ppermute(corner_mine, "row", [(0, shift)])
@@ -548,10 +679,11 @@
     out = None
     for step, part in enumerate(parts):
         if step == 2:
-            arrived.append(exchange(parts[3], arrived[2], out))
+            arrived.append(exchange(packed(parts[3]), arrived[2], out))
         out = finish(
             part,
-            [counts[a] for a in part],
+            [shared[a] for a in part],
+            [edge_of.get(a) for a in part],
             row_size,
             col_size,
             ids,
@@ -561,6 +693,7 @@
             high,
             low,
             kids,
+            edge,
             out,
         )
     return out.reshape(row_tiles, 1, width, col_tiles, 1, width)

time: 577 us -> 526 us (0.912)
  waiting for transfers between devices: 258 us -> 232 us
  starting transfers between devices: 82.4 us -> 61.8 us
  blocking collectives: 20.1 us -> 5.04 us
  loops' own time: 0.01 us -> 8.63 us
    ppermute x3, waiting for transfers between devices: 34.7 us -> 0.01 us  [on_device(): lax.ppermute(raw, 'col', across_col(k))]
    all_to_all x4, waiting for transfers between devices: 73.8 us -> 45.2 us  [exchange(): lax.all_to_all(blocks, 'col', split_axis=0, concat_axis=0, tiled=True)]
    ppermute x9 -> x12, waiting for transfers between devices: 142 us -> 168 us  [the longest x1 92.4 us: on_device(): other = lax.ppermute(jnp.stack(same), 'col', across_col(1))]
    pallas_call x4 -> x6, Pallas kernels: 48.2 us -> 63.9 us  [the longest x4 56.4 us: finish(): pl.pallas_call(functools.partial(finish_kernel, depths, shared, edges, ro...]
    all_gather x1, blocking collectives: 20.1 us -> 5.04 us  [on_device(): meta = lax.all_gather(meta, 'row', axis=0, tiled=True)]
    ppermute x3, starting transfers between devices: 18.2 us -> 6.79 us  [on_device(): lax.ppermute(raw, 'col', across_col(k))]
    another operation x1, loops' own time: 0.01 us -> 8.63 us  [on_device(): jax.scipy.linalg.solve_triangular(factor, jnp.eye(width, dtype=jnp.float3...]
    ppermute x3, starting transfers between devices: 8.36 us -> 1.77 us  [on_device(): lax.ppermute(moved[shift], 'row', along_row(shift))]
  transfers between devices with their start and end apart: 28 -> 31, of which waited for: 10 -> 13; matrix products, arithmetic and copies ran while one was open for 14% -> 15% of each run, Pallas kernels for 16% -> 20%
where the time goes in v3:
time: 526 us; the launch traced here: 516 us
  waiting for transfers between devices  232 us (44%)
  Pallas kernels  120 us (23%)
  other arithmetic  65.4 us (12%)
  starting transfers between devices  61.8 us (12%)
  local copies, waits for them, and re-layouts  17.7 us (3%)
  loops' own time  8.63 us (2%)
    ppermute x1, waiting for transfers between devices, on_device(): other = lax.ppermute(jnp.stack(same), 'col', across_col(1))  92.4 us
    pallas_call x4, Pallas kernels, finish(): pl.pallas_call(functools.partial(finish_kernel, depths, shared, edges, ro...  56.4 us
    ppermute x7, waiting for transfers between devices, send_edge(): return lax.ppermute(value, ('row', 'col'), steps)  55.3 us
    all_to_all x4, waiting for transfers between devices, exchange(): lax.all_to_all(blocks, 'col', split_axis=0, concat_axis=0, tiled=True)  45.2 us
    another operation x6, other arithmetic, on_device(): factor = jnp.linalg.cholesky(corner)  34 us
    all_to_all x4, starting transfers between devices, exchange(): lax.all_to_all(blocks, 'col', split_axis=0, concat_axis=0, tiled=True)  28 us
    pallas_call x4, Pallas kernels, pack(): pl.pallas_call(functools.partial(pack_kernel, depths, counts), out_shape=...  23.5 us
    another operation x4, other arithmetic, on_device(): jax.scipy.linalg.solve_triangular(factor, jnp.eye(width, dtype=jnp.float3...  21.1 us
  transfers between devices with their start and end apart: 31, of which 13 were waited for; matrix products, arithmetic and copies ran while one was open for 15% of the time, Pallas kernels for 20%

profile of v3, /device:TPU:6, one launch (start us, length us, event | category | flops | bytes accessed | tf_op | source)
XLA Modules:
  0.0 515.5 jit_solution(13642192941479194647)
XLA Ops:
  1.2 8.5 %move_tiles.1 = (f32[2,256,256]{2,1,0:T(8,128)}, f32[2,256,256]{2,1,0:T(8,128)}, f32[2,256,256]{2,1,0:T(8,128)}, f32[2,256,256]{2,1,0:T(8,128)}, f32[2,4,80,256]...) custom-call(s32[2]{0:T(128)} %pad_add_fusion.ids_ref, ...), custom_call_target="tpu_custom_call" | custom-call | tf_op jit(solution)/shard_map/move_tiles/pallas_call | solution.py:95
  22.2 7.5 %pack.4 = f32[8,21,32,256]{3,2,1,0:T(8,128)} custom-call(f32[16,1,32,8,8,256]{5,4,3,2,1,0:T(8,128)} %front_ref.6), custom_call_target="tpu_custom_call" | custom-call | tf_op jit(solution)/shard_map/pack/pallas_call | solution.py:332
  43.2 10.3 %collective-permute-done.8.rest_4_ = f32[8,32,256]{2,1,0:T(8,128)S(1)} collective-permute-done((f32[8,32,256]{2,1,0:T(8,128)}, f32[8,32,256]{2,1,0:T(8,128)S(1)}, u32[]{:S(2)}, u32[]{:S(2)}) %collective-permute-start.8) | collective-permute-done | bytes 262176 | tf_op jit(solution)/shard_map/ppermute | solution.py:617
  53.6 6.3 %collective-permute-done.9.rest_5_ = f32[8,32,256]{2,1,0:T(8,128)S(1)} collective-permute-done((f32[8,32,256]{2,1,0:T(8,128)}, f32[8,32,256]{2,1,0:T(8,128)S(1)}, u32[]{:S(2)}, u32[]{:S(2)}) %collective-permute-start.9) | collective-permute-done | bytes 262176 | tf_op jit(solution)/shard_map/ppermute | solution.py:617
  59.9 12.1 %all-to-all-start = ((f32[8,7,32,256]{3,2,1,0:T(8,128)}), f32[8,7,32,256]{3,2,1,0:T(8,128)S(1)}, u32[]{:S(2)}, u32[]{:S(2)}) async-start(f32[8,7,32,256]{3,2,1,0:T(8,128)} %pack.7), calls=%async_computation | async-start | bytes 3670016 | tf_op jit(solution)/shard_map/all_to_all | solution.py:583
  75.9 20.0 %collective-permute-done.3 = f32[4,80,256]{2,1,0:T(8,128)S(1)} collective-permute-done((f32[4,80,256]{2,1,0:T(8,128)S(1)}, f32[4,80,256]{2,1,0:T(8,128)S(1)}, u32[]{:S(2)}, u32[]{:S(2)}) %collective-permute-start.3) | collective-permute-done | bytes 327712 | tf_op jit(solution)/shard_map/ppermute | solution.py:633
  121.7 32.1 %collective-permute-done.15.rest_2_ = f32[8,32,256]{2,1,0:T(8,128)S(1)} collective-permute-done((f32[8,32,256]{2,1,0:T(8,128)}, f32[8,32,256]{2,1,0:T(8,128)S(1)}, u32[]{:S(2)}, u32[]{:S(2)}) %collective-permute-start.15) | collective-permute-done | bytes 262176 | tf_op jit(solution)/shard_map/ppermute | solution.py:617
  162.3 6.3 %all-to-all-start.1 = ((f32[8,21,32,256]{3,2,1,0:T(8,128)}), f32[8,21,32,256]{3,2,1,0:T(8,128)}, u32[]{:S(2)}, u32[]{:S(2)}) async-start(f32[8,21,32,256]{3,2,1,0:T(8,128)} %pack.4), calls=%async_computation.1 | async-start | bytes 11010048 | tf_op jit(solution)/shard_map/all_to_all | solution.py:583
  170.2 10.2 %pack.6 = f32[8,31,32,256]{3,2,1,0:T(8,128)} custom-call(f32[16,1,32,8,8,256]{5,4,3,2,1,0:T(8,128)} %front_ref.6), custom_call_target="tpu_custom_call" | custom-call | tf_op jit(solution)/shard_map/pack/pallas_call | solution.py:332
  180.4 92.4 %collective-permute-done.17.refs_4_ = f32[4,16,32,256]{3,2,1,0:T(8,128)} collective-permute-done((f32[4,16,32,256]{3,2,1,0:T(8,128)S(1)}, f32[4,16,32,256]{3,2,1,0:T(8,128)}, u32[]{:S(2)}, u32[]{:S(2)}) %collective-permute-start.17) | collective-permute-done | bytes 2097184 | tf_op jit(solution)/shard_map/ppermute | solution.py:643
  272.9 17.1 %all-to-all-done.1.recv_ref = f32[8,21,32,256]{3,2,1,0:T(8,128)} async-done(((f32[8,21,32,256]{3,2,1,0:T(8,128)}), f32[8,21,32,256]{3,2,1,0:T(8,128)}, u32[]{:S(2)}, u32[]{:S(2)}) %all-to-all-start.1) | async-done | bytes 5505056 | tf_op jit(solution)/shard_map/all_to_all | solution.py:583
  299.9 9.3 %collective-permute-done.24 = f32[2,256,256]{2,1,0:T(8,128)} collective-permute-done((f32[2,256,256]{2,1,0:T(8,128)}, f32[2,256,256]{2,1,0:T(8,128)}, u32[]{:S(2)}, u32[]{:S(2)}) %collective-permute-start.24) | collective-permute-done | bytes 524320 | tf_op jit(solution)/shard_map/ppermute | solution.py:651
  326.7 6.6 %collective-permute-done.19 = f32[256,256]{1,0:T(8,128)S(1)} collective-permute-done((f32[256,256]{1,0:T(8,128)S(1)}, f32[256,256]{1,0:T(8,128)S(1)}, u32[]{:S(2)}, u32[]{:S(2)}) %collective-permute-start.19) | collective-permute-done | bytes 262176 | tf_op jit(solution)/shard_map/ppermute | solution.py:657
  333.7 11.7 %cholesky.49 = f32[128,128]{1,0:T(8,128)S(1)} custom-call(f32[128,128]{1,0:T(8,128)S(1)} %cholesky.115), custom_call_target="Cholesky" | custom-call | tf_op jit(solution)/shard_map/jit(cholesky)/cholesky | solution.py:659
  345.5 9.8 %custom-call.15 = f32[1,128,128]{1,2,0:T(8,128)S(1)} custom-call(f32[1,128,128]{2,1,0:T(8,128)S(1)} %get-tuple-element.110), custom_call_target="InvertDiagBlocksLowerTriangular" | custom-call | tf_op jit(solution)/shard_map/jit(cholesky)/cholesky | solution.py:659
  355.8 11.7 %cholesky.103 = f32[128,128]{1,0:T(8,128)S(1)} custom-call(f32[128,128]{1,0:T(8,128)S(1)} %convolution_subtract_fusion.1), custom_call_target="Cholesky" | custom-call | tf_op jit(solution)/shard_map/jit(cholesky)/cholesky | solution.py:659
  370.4 12.9 %while.1 = (s32[]{:T(128)}, f32[256,256]{1,0:T(8,128)S(1)}, s32[2,2]{1,0:T(2,128)S(1)}, f32[2,128,128]{2,1,0:T(8,128)S(1)}, s32[]{:T(128)}) while((s32[]{:T(128)}, f32[256,256]{1,0:T(8,128)S(1)}, s32[2,2]{1,0:T(2,128)S(1)}, f32[2,128,128]{2,1,0:T(8,128)S(1)}, s32[]{:T(128)}) %tuple.51), condition=%wide.while_cond, body=%wide.while_body.sunk | while | flops 2 | bytes 131181 | solution.py:660
  383.3 19.7 %custom-call.16 = f32[2,128,128]{1,2,0:T(8,128)S(1)} custom-call(f32[2,128,128]{2,1,0:T(8,128)S(1)} %get-tuple-element.90), custom_call_target="InvertDiagBlocksLowerTriangular" | custom-call | tf_op jit(solution)/shard_map/jit(_solve_triangular)/triangular_solve | solution.py:660
  409.8 15.4 %panels.1 = (f32[16,256,256]{2,1,0:T(8,128)}, bf16[8,256,256]{2,1,0:T(8,128)(2,1)}, bf16[8,256,256]{2,1,0:T(8,128)(2,1)}) custom-call(s32[2]{0:T(128)} %pad_add_fusion.ids_ref, f32[256,256]{1,0:T(8,128)} %pad_maximum_fusion.1.inverse_ref, f32[256,256]{1,0:T(8,128)} %get-tuple-element.100.factor_ref, f32[8,16,32,256]{3,2,1,0:T(8,128)} %order_rows.1.rows_ref, ...), custom_call_target="tpu_custom_call" | custom-call | tf_op jit(solution)/shard_map/panels/pallas_call | solution.py:269
  425.3 7.1 %finish.4.rest_8_ = f32[16,4096,128]{2,1,0:T(8,128)} custom-call(s32[2]{0:T(128)} %pad_add_fusion.ids_ref, s32[2,8]{1,0:T(2,128)} %locate.1.own_ref, f32[8,7,32,256]{3,2,1,0:T(8,128)} %copy-done.1, f32[16,256,256]{2,1,0:T(8,128)} %get-tuple-element.70.rows_ref, bf16[8,256,256]{2,1,0:T(8,128)(2,1)} %get-tuple-element.71.high_ref, ...), custom_call_target="tpu_custom_call" | custom-call | tf_op jit(solution)/shard_map/finish/pallas_call | solution.py:531
  432.4 11.5 %finish.5.rest_8_ = f32[16,4096,128]{2,1,0:T(8,128)} custom-call(s32[2]{0:T(128)} %pad_add_fusion.ids_ref, s32[2,8]{1,0:T(2,128)} %locate.1.own_ref, f32[8,21,32,256]{3,2,1,0:T(8,128)} %all-to-all-done.1.recv_ref, f32[16,256,256]{2,1,0:T(8,128)} %get-tuple-element.70.rows_ref, ...), custom_call_target="tpu_custom_call", output_to_operand_aliasing={{}: (15, {})} | custom-call | tf_op jit(solution)/shard_map/finish/pallas_call | solution.py:531
  443.9 28.1 %all-to-all-done.2.recv_ref = f32[8,31,32,256]{3,2,1,0:T(8,128)} async-done(((f32[8,31,32,256]{3,2,1,0:T(8,128)}), f32[8,31,32,256]{3,2,1,0:T(8,128)}, u32[]{:S(2)}, u32[]{:S(2)}) %all-to-all-start.2) | async-done | bytes 8126496 | tf_op jit(solution)/shard_map/all_to_all | solution.py:583
  476.2 31.2 %finish.6.rest_8_ = f32[16,4096,128]{2,1,0:T(8,128)} custom-call(s32[2]{0:T(128)} %pad_add_fusion.ids_ref, s32[2,8]{1,0:T(2,128)} %locate.1.own_ref, f32[8,31,32,256]{3,2,1,0:T(8,128)} %all-to-all-done.2.recv_ref, f32[16,256,256]{2,1,0:T(8,128)} %get-tuple-element.70.rows_ref, ...), custom_call_target="tpu_custom_call", output_to_operand_aliasing={{}: (15, {})} | custom-call | tf_op jit(solution)/shard_map/finish/pallas_call | solution.py:531
  508.5 6.6 %finish.7 = f32[16,4096,128]{2,1,0:T(8,128)} custom-call(s32[2]{0:T(128)} %pad_add_fusion.ids_ref, s32[2,8]{1,0:T(2,128)} %locate.1.own_ref, f32[8,5,32,256]{3,2,1,0:T(8,128)} %copy-done.2, f32[16,256,256]{2,1,0:T(8,128)} %get-tuple-element.70.rows_ref, bf16[8,256,256]{2,1,0:T(8,128)(2,1)} %get-tuple-element.71.high_ref, ...), custom_call_target="tpu_custom_call", output_to_operand_aliasing={{}: (15, {})} | custom-call | tf_op jit(solution)/shard_map/finish/pallas_call | solution.py:531
  (146 shorter events, 112.1 us)
Async XLA Ops:
  11.2 32.0 %collective-permute-start.2 = (f32[2,4,80,256]{3,2,1,0:T(8,128)}, f32[2,4,80,256]{3,2,1,0:T(8,128)S(1)}, u32[]{:S(2)}, u32[]{:S(2)}) collective-permute-start(f32[2,4,80,256]{3,2,1,0:T(8,128)} %get-tuple-element.46), channel_id=1, source_target_pairs={{0,6},{8,14},{16,22},{24,30}} | collective-permute-start | bytes 1966088 | tf_op jit(solution)/shard_map/ppermute | solution.py:606
  16.2 27.0 %collective-permute-start.10 = (f32[8,32,256]{2,1,0:T(8,128)}, f32[8,32,256]{2,1,0:T(8,128)S(1)}, u32[]{:S(2)}, u32[]{:S(2)}) collective-permute-start(f32[8,32,256]{2,1,0:T(8,128)} %get-tuple-element.59), channel_id=1, source_target_pairs={{6,0},{14,8},{15,9},{20,18},{22,16},{23,17},{28,26},{29,27},{30,24... | collective-permute-start | bytes 786440 | tf_op jit(solution)/shard_map/ppermute | solution.py:617
  17.5 25.7 %collective-permute-start.11 = (f32[8,32,256]{2,1,0:T(8,128)}, f32[8,32,256]{2,1,0:T(8,128)S(1)}, u32[]{:S(2)}, u32[]{:S(2)}) collective-permute-start(f32[8,32,256]{2,1,0:T(8,128)} %get-tuple-element.60), channel_id=1, source_target_pairs={{7,0},{14,9},{15,8},{21,18},{22,17},{23,16},{28,27},{29,26},{30,25... | collective-permute-start | bytes 786440 | tf_op jit(solution)/shard_map/ppermute | solution.py:617
  19.6 33.9 %collective-permute-start.8 = (f32[8,32,256]{2,1,0:T(8,128)}, f32[8,32,256]{2,1,0:T(8,128)S(1)}, u32[]{:S(2)}, u32[]{:S(2)}) collective-permute-start(f32[8,32,256]{2,1,0:T(8,128)} %get-tuple-element.57), channel_id=1, source_target_pairs={{4,0},{12,8},{13,9},{20,16},{21,17},{22,18},{28,24},{29,25},{30,26... | collective-permute-start | bytes 786440 | tf_op jit(solution)/shard_map/ppermute | solution.py:617
  20.9 39.0 %collective-permute-start.9 = (f32[8,32,256]{2,1,0:T(8,128)}, f32[8,32,256]{2,1,0:T(8,128)S(1)}, u32[]{:S(2)}, u32[]{:S(2)}) collective-permute-start(f32[8,32,256]{2,1,0:T(8,128)} %get-tuple-element.58), channel_id=1, source_target_pairs={{5,0},{12,9},{13,8},{20,17},{21,16},{23,18},{28,25},{29,24},{30,27... | collective-permute-start | bytes 786440 | tf_op jit(solution)/shard_map/ppermute | solution.py:617
  59.9 101.1 %all-to-all-start = ((f32[8,7,32,256]{3,2,1,0:T(8,128)}), f32[8,7,32,256]{3,2,1,0:T(8,128)S(1)}, u32[]{:S(2)}, u32[]{:S(2)}) async-start(f32[8,7,32,256]{3,2,1,0:T(8,128)} %pack.7), calls=%async_computation | async-start | bytes 3670016 | tf_op jit(solution)/shard_map/all_to_all | solution.py:583
  74.6 21.3 %collective-permute-start.3 = (f32[4,80,256]{2,1,0:T(8,128)S(1)}, f32[4,80,256]{2,1,0:T(8,128)S(1)}, u32[]{:S(2)}, u32[]{:S(2)}) collective-permute-start(f32[4,80,256]{2,1,0:T(8,128)S(1)} %slice_bitcast_fusion), channel_id=1, source_target_pairs={{0,1},{2,3},{4,5},{6,7},{8,9},{10,11},{12,13},{14,15},{16,17},{18,... | collective-permute-start | bytes 983048 | tf_op jit(solution)/shard_map/ppermute | solution.py:633
  107.9 51.5 %collective-permute-start.7 = (f32[16,32,256]{2,1,0:T(8,128)}, f32[16,32,256]{2,1,0:T(8,128)S(1)}, u32[]{:S(2)}, u32[]{:S(2)}) collective-permute-start(f32[16,32,256]{2,1,0:T(8,128)} %lead_rows.1.refs_0_), channel_id=1, source_target_pairs={{0,2},{1,3},{2,0},{3,1},{4,6},{5,7},{6,4},{7,5},{8,10},{9,11},{10,... | collective-permute-start | bytes 1572872 | tf_op jit(solution)/shard_map/ppermute | solution.py:640
  112.0 47.4 %collective-permute-start.12 = (f32[16,32,256]{2,1,0:T(8,128)}, f32[16,32,256]{2,1,0:T(8,128)S(1)}, u32[]{:S(2)}, u32[]{:S(2)}) collective-permute-start(f32[16,32,256]{2,1,0:T(8,128)} %lead_rows.1.refs_0_), channel_id=1, source_target_pairs={{0,4},{1,5},{2,6},{3,7},{4,0},{5,1},{6,2},{7,3},{8,12},{9,13},{10,... | collective-permute-start | bytes 1572872 | tf_op jit(solution)/shard_map/ppermute | solution.py:640
  113.3 47.7 %collective-permute-start.13 = (f32[16,32,256]{2,1,0:T(8,128)}, f32[16,32,256]{2,1,0:T(8,128)}, u32[]{:S(2)}, u32[]{:S(2)}) collective-permute-start(f32[16,32,256]{2,1,0:T(8,128)} %lead_rows.1.refs_0_), channel_id=1, source_target_pairs={{0,6},{1,7},{2,4},{3,5},{4,2},{5,3},{6,0},{7,1},{8,14},{9,15},{10,... | collective-permute-start | bytes 1572872 | tf_op jit(solution)/shard_map/ppermute | solution.py:640
  114.7 39.1 %collective-permute-start.15 = (f32[8,32,256]{2,1,0:T(8,128)}, f32[8,32,256]{2,1,0:T(8,128)S(1)}, u32[]{:S(2)}, u32[]{:S(2)}) collective-permute-start(f32[8,32,256]{2,1,0:T(8,128)} %get-tuple-element.65), channel_id=1, source_target_pairs={{2,0},{10,8},{11,9},{16,18},{18,16},{19,17},{24,26},{25,27},{26,24... | collective-permute-start | bytes 786440 | tf_op jit(solution)/shard_map/ppermute | solution.py:617
  116.9 42.5 %collective-permute-start.16 = (f32[8,32,256]{2,1,0:T(8,128)}, f32[8,32,256]{2,1,0:T(8,128)S(1)}, u32[]{:S(2)}, u32[]{:S(2)}) collective-permute-start(f32[8,32,256]{2,1,0:T(8,128)} %get-tuple-element.67), channel_id=1, source_target_pairs={{3,0},{10,9},{11,8},{17,18},{18,17},{19,16},{24,27},{25,26},{26,25... | collective-permute-start | bytes 786440 | tf_op jit(solution)/shard_map/ppermute | solution.py:617
  162.3 127.7 %all-to-all-start.1 = ((f32[8,21,32,256]{3,2,1,0:T(8,128)}), f32[8,21,32,256]{3,2,1,0:T(8,128)}, u32[]{:S(2)}, u32[]{:S(2)}) async-start(f32[8,21,32,256]{3,2,1,0:T(8,128)} %pack.4), calls=%async_computation.1 | async-start | bytes 11010048 | tf_op jit(solution)/shard_map/all_to_all | solution.py:583
  170.1 102.7 %collective-permute-start.17 = (f32[4,16,32,256]{3,2,1,0:T(8,128)S(1)}, f32[4,16,32,256]{3,2,1,0:T(8,128)}, u32[]{:S(2)}, u32[]{:S(2)}) collective-permute-start(f32[4,16,32,256]{3,2,1,0:T(8,128)S(1)} %pad_maximum_fusion), channel_id=1, source_target_pairs={{0,1},{1,0},{2,3},{3,2},{4,5},{5,4},{6,7},{7,6},{8,9},{9,8},{10,11... | collective-permute-start | bytes 6291464 | tf_op jit(solution)/shard_map/ppermute | solution.py:643
  289.9 182.1 %all-to-all-start.2 = ((f32[8,31,32,256]{3,2,1,0:T(8,128)}), f32[8,31,32,256]{3,2,1,0:T(8,128)}, u32[]{:S(2)}, u32[]{:S(2)}) async-start(f32[8,31,32,256]{3,2,1,0:T(8,128)} %pack.6), calls=%async_computation.2 | async-start | bytes 16252928 | tf_op jit(solution)/shard_map/all_to_all | solution.py:583
  295.3 14.0 %collective-permute-start.24 = (f32[2,256,256]{2,1,0:T(8,128)}, f32[2,256,256]{2,1,0:T(8,128)}, u32[]{:S(2)}, u32[]{:S(2)}) collective-permute-start(f32[2,256,256]{2,1,0:T(8,128)} %get-tuple-element.78), channel_id=1, source_target_pairs={{0,8},{8,16},{16,24},{24,0},{1,9},{9,17},{17,25},{25,1},{2,10},{10... | collective-permute-start | bytes 1572872 | tf_op jit(solution)/shard_map/ppermute | solution.py:651
  295.3 15.1 %collective-permute-start.25 = (f32[2,256,256]{2,1,0:T(8,128)}, f32[2,256,256]{2,1,0:T(8,128)S(1)}, u32[]{:S(2)}, u32[]{:S(2)}) collective-permute-start(f32[2,256,256]{2,1,0:T(8,128)} %get-tuple-element.79), channel_id=1, source_target_pairs={{0,16},{8,24},{16,0},{24,8},{1,17},{9,25},{17,1},{25,9},{2,18},{10... | collective-permute-start | bytes 1572872 | tf_op jit(solution)/shard_map/ppermute | solution.py:651
  295.3 23.3 %collective-permute-start.26 = (f32[2,256,256]{2,1,0:T(8,128)}, f32[2,256,256]{2,1,0:T(8,128)S(1)}, u32[]{:S(2)}, u32[]{:S(2)}) collective-permute-start(f32[2,256,256]{2,1,0:T(8,128)} %get-tuple-element.80), channel_id=1, source_target_pairs={{0,24},{8,0},{16,8},{24,16},{1,25},{9,1},{17,9},{25,17},{2,26},{10... | collective-permute-start | bytes 1572872 | tf_op jit(solution)/shard_map/ppermute | solution.py:651
  316.6 16.7 %collective-permute-start.19 = (f32[256,256]{1,0:T(8,128)S(1)}, f32[256,256]{1,0:T(8,128)S(1)}, u32[]{:S(2)}, u32[]{:S(2)}) collective-permute-start(f32[256,256]{1,0:T(8,128)S(1)} %bitcast.83), channel_id=1, source_target_pairs={{0,16},{1,17},{2,18},{3,19},{4,20},{5,21},{6,22},{7,23}} | collective-permute-start | bytes 786440 | tf_op jit(solution)/shard_map/ppermute | solution.py:657
  317.9 15.4 %collective-permute-start.20 = (f32[256,256]{1,0:T(8,128)S(1)}, f32[256,256]{1,0:T(8,128)S(1)}, u32[]{:S(2)}, u32[]{:S(2)}) collective-permute-start(f32[256,256]{1,0:T(8,128)S(1)} %bitcast.84), channel_id=1, source_target_pairs={{0,24},{1,25},{2,26},{3,27},{4,28},{5,29},{6,30},{7,31}} | collective-permute-start | bytes 786440 | tf_op jit(solution)/shard_map/ppermute | solution.py:657
  322.6 82.0 %collective-permute-start.21 = (f32[8,8,32,256]{3,2,1,0:T(8,128)}, f32[8,8,32,256]{3,2,1,0:T(8,128)}, u32[]{:S(2)}, u32[]{:S(2)}) collective-permute-start(f32[8,8,32,256]{3,2,1,0:T(8,128)} %dynamic-slice_bitcast_fusion), channel_id=1, source_target_pairs={{0,8},{9,17},{18,26},{27,3},{4,12},{13,21},{22,30},{31,7}} | collective-permute-start | bytes 6291464 | tf_op jit(solution)/shard_map/ppermute | solution.py:676
  323.9 80.7 %collective-permute-start.22 = (f32[8,8,32,256]{3,2,1,0:T(8,128)}, f32[8,8,32,256]{3,2,1,0:T(8,128)S(1)}, u32[]{:S(2)}, u32[]{:S(2)}) collective-permute-start(f32[8,8,32,256]{3,2,1,0:T(8,128)} %dynamic-slice_bitcast_fusion), channel_id=1, source_target_pairs={{0,16},{9,25},{18,2},{27,11},{4,20},{13,29},{22,6},{31,15}} | collective-permute-start | bytes 6291464 | tf_op jit(solution)/shard_map/ppermute | solution.py:676
  324.7 79.9 %collective-permute-start.23 = (f32[8,8,32,256]{3,2,1,0:T(8,128)}, f32[8,8,32,256]{3,2,1,0:T(8,128)}, u32[]{:S(2)}, u32[]{:S(2)}) collective-permute-start(f32[8,8,32,256]{3,2,1,0:T(8,128)} %dynamic-slice_bitcast_fusion), channel_id=1, source_target_pairs={{0,24},{9,1},{18,10},{27,19},{4,28},{13,5},{22,14},{31,23}} | collective-permute-start | bytes 6291464 | tf_op jit(solution)/shard_map/ppermute | solution.py:676
  472.0 35.3 %all-to-all-start.3 = ((f32[8,5,32,256]{3,2,1,0:T(8,128)}), f32[8,5,32,256]{3,2,1,0:T(8,128)S(1)}, u32[]{:S(2)}, u32[]{:S(2)}) async-start(f32[8,5,32,256]{3,2,1,0:T(8,128)} %pack.5), calls=%async_computation.3 | async-start | bytes 2621440 | tf_op jit(solution)/shard_map/all_to_all | solution.py:583
  (30 other events, 300.8 us)
